TPU v7x, 256 devices: a whole 4x4x8 slice. The times are simulated.
256 devices in a mesh: seq: 32 (over x, z), head: 8 (over y, core).
Axes of the slice: x: 4, y: 4, z: 8, core: 2. Of those that a mesh axis runs over, the one named last changes fastest.
Arguments:
- tokens: bfloat16 [8192, 3072], P('seq', 'head'), may hold values from -6 to 6
- norm_gain: float32 [3072], replicated, may hold values from 0.1 to 1.9
- w_query: bfloat16 [3072, 3072], P(None, 'head'), may hold values from -0.109375 to 0.109375
- w_key: bfloat16 [3072, 1024], P(None, 'head'), may hold values from -0.3125 to 0.3125
- w_value: bfloat16 [3072, 1024], P(None, 'head'), may hold values from -0.109375 to 0.109375
- w_out: bfloat16 [3072, 3072], P('head'), may hold values from -0.109375 to 0.109375
- keys_cache: bfloat16 [65536, 1024], P('seq', 'head'), may hold values from -120 to 120
- values_cache: bfloat16 [65536, 1024], P('seq', 'head'), may hold values from -6 to 6
- cached_lengths: int32 [4], replicated, may hold values from 0 to 14336, as said below
- rope_offsets: int32 [4], replicated, may hold values from 0 to 8191
Outputs:
- attn_proj: bfloat16 [8192, 3072], P('seq', 'head')
- keys_updated: bfloat16 [65536, 1024], P('seq', 'head')
- values_updated: bfloat16 [65536, 1024], P('seq', 'head')
Inputs may be any that keep to these rules, and one draw needn't show every extreme that they name: `cached_lengths`: in every draw one request has exactly 14336 cached tokens.
All inputs are finite; a program needn't handle non-finite values.
Results may differ from a plain program's by a relative error of at most 0.02.
Values may be sent and summed in bfloat16 or wider, within the bound.
A program may use at most 128 MiB of HBM per device.

v0:
```python
import math

import jax
import jax.numpy as jnp
from jax import lax
from jax.sharding import PartitionSpec as P

HD = 128


rope_base = 500000.0
neg_large = -1e30


def shifted(shard, axis, by):
    devices = lax.axis_size(axis)
    return lax.ppermute(shard, axis, [(i, (i + by) % devices) for i in range(devices)])


def rotate(vectors, positions):
    half_width = vectors.shape[-1] // 2
    frequency = rope_base ** (-jnp.arange(half_width, dtype=jnp.float32) * 2.0 / vectors.shape[-1])
    angles = positions.astype(jnp.float32)[:, None] * frequency[None, :]
    cosine = jnp.cos(angles)[:, None, :]
    sine_part = jnp.sin(angles)[:, None, :]
    first_half = vectors[..., :half_width]
    second_half = vectors[..., half_width:]
    return jnp.concatenate(
        [
            first_half * cosine - second_half * sine_part,
            second_half * cosine + first_half * sine_part,
        ],
        -1,
    )


def shards(
    tokens,
    norm_gain,
    w_query,
    w_key,
    w_value,
    w_out,
    keys_cache,
    values_cache,
    cached_lengths,
    rope_offsets,
):
    gathered = lax.all_gather(tokens, "head", axis=1, tiled=True)
    row_count = gathered.shape[0]
    requests = cached_lengths.shape[0]
    groups = lax.axis_size("seq") // requests
    member = lax.axis_index("seq")
    request = member % requests
    position_in = member // requests
    length = lax.dynamic_index_in_dim(cached_lengths, request, 0, False)
    offset = lax.dynamic_index_in_dim(rope_offsets, request, 0, False)
    widened = gathered.astype(jnp.float32)
    normed = (
        widened * lax.rsqrt(jnp.mean(widened * widened, -1, keepdims=True) + 1e-05) * norm_gain
    ).astype(jnp.bfloat16)
    index_new = position_in * row_count + jnp.arange(row_count, dtype=jnp.int32)
    positions = offset + length + index_new
    kv_heads = w_key.shape[1] // HD
    q_heads = w_query.shape[1] // HD
    repeat = q_heads // kv_heads
    queries = rotate(
        jnp.dot(normed, w_query, preferred_element_type=jnp.float32).reshape(
            row_count, q_heads, HD
        ),
        positions,
    ).astype(jnp.bfloat16)
    new_keys = (
        rotate(
            jnp.dot(normed, w_key, preferred_element_type=jnp.float32).reshape(
                row_count, kv_heads, HD
            ),
            positions,
        )
        .astype(jnp.bfloat16)
        .reshape(row_count, kv_heads * HD)
    )
    new_values = jnp.dot(normed, w_value, preferred_element_type=jnp.float32).astype(jnp.bfloat16)
    grouped = (
        queries.reshape(row_count, kv_heads, repeat, HD)
        .transpose(1, 2, 0, 3)
        .reshape(kv_heads, repeat * row_count, HD)
    )
    slab_rows = keys_cache.shape[0]
    score_scale = 1.0 / math.sqrt(HD)

    def attend(softmax_state, query_group, key_block, value_block, visible):
        running_max, denominator, accumulated = softmax_state
        scores = (
            jnp.einsum(
                "gqd,kgd->gqk",
                query_group,
                key_block.reshape(-1, kv_heads, HD),
                preferred_element_type=jnp.float32,
            )
            * score_scale
        )
        masked = jnp.where(visible, scores, neg_large)
        new_max = jnp.maximum(running_max, jnp.max(masked, -1))
        weights = jnp.where(visible, jnp.exp(masked - new_max[..., None]), 0.0)
        factor = jnp.exp(running_max - new_max)
        denominator = denominator * factor + jnp.sum(weights, -1)
        accumulated = accumulated * factor[..., None] + jnp.einsum(
            "gqk,kgd->gqd",
            weights.astype(jnp.bfloat16),
            value_block.reshape(-1, kv_heads, HD),
            preferred_element_type=jnp.float32,
        )
        return (new_max, denominator, accumulated)

    def attend_pair(
        softmax_state,
        query_anchor,
        query_group,
        slab_keys,
        slab_values,
        slab_source,
        fresh_keys,
        fresh_values,
        fresh_source,
    ):
        query_index = jnp.tile(
            query_anchor * row_count + jnp.arange(row_count, dtype=jnp.int32), repeat
        )
        slots = slab_source * slab_rows + jnp.arange(slab_rows, dtype=jnp.int32)
        old_visible = (slots < length)[None, None, :]
        fresh_index = fresh_source * row_count + jnp.arange(row_count, dtype=jnp.int32)
        fresh_visible = (fresh_index[None, :] <= query_index[:, None])[None]
        softmax_state = attend(softmax_state, query_group, slab_keys, slab_values, old_visible)
        softmax_state = attend(softmax_state, query_group, fresh_keys, fresh_values, fresh_visible)
        return softmax_state

    def write_fresh(out_keys, out_values, fresh_keys, fresh_values, fresh_source):
        fresh_index = fresh_source * row_count + jnp.arange(row_count, dtype=jnp.int32)
        local_slot = length + fresh_index - position_in * slab_rows
        target = jnp.where((local_slot >= 0) & (local_slot < slab_rows), local_slot, slab_rows)
        out_keys = out_keys.at[target].set(fresh_keys, mode="drop")
        out_values = out_values.at[target].set(fresh_values, mode="drop")
        return (out_keys, out_values)

    def absorb(loop_carry, incoming, source):
        softmax_state, out_keys, out_values = loop_carry
        fresh_keys = incoming[0, slab_rows:]
        fresh_values = incoming[1, slab_rows:]
        softmax_state = attend_pair(
            softmax_state,
            position_in,
            grouped,
            incoming[0, :slab_rows],
            incoming[1, :slab_rows],
            source,
            fresh_keys,
            fresh_values,
            source,
        )
        out_keys, out_values = write_fresh(out_keys, out_values, fresh_keys, fresh_values, source)
        return (softmax_state, out_keys, out_values)

    start_state = (
        jnp.full((kv_heads, repeat * row_count), neg_large, jnp.float32),
        jnp.zeros((kv_heads, repeat * row_count), jnp.float32),
        jnp.zeros((kv_heads, repeat * row_count, HD), jnp.float32),
    )
    outgoing = jnp.stack(
        [
            jnp.concatenate([keys_cache, new_keys], 0),
            jnp.concatenate([values_cache, new_values], 0),
        ],
        0,
    )
    loop_carry = absorb((start_state, keys_cache, values_cache), outgoing, position_in)

    def cycle_step(cycle_turn, cycle_carry):
        held_blocks, inner_carry = cycle_carry
        held_blocks = shifted(held_blocks, "seq", requests)
        source = (position_in - cycle_turn) % groups
        return (held_blocks, absorb(inner_carry, held_blocks, source))

    unused, loop_carry = lax.fori_loop(1, groups, cycle_step, (outgoing, loop_carry))
    final_state, keys_updated, values_updated = loop_carry
    running_max, denominator, accumulated = final_state
    attended = (
        (accumulated / denominator[..., None])
        .reshape(kv_heads, repeat, row_count, HD)
        .transpose(2, 0, 1, 3)
        .reshape(row_count, q_heads * HD)
        .astype(jnp.bfloat16)
    )
    partial_value = jnp.dot(attended, w_out, preferred_element_type=jnp.float32)
    summed = lax.psum(partial_value.astype(jnp.bfloat16), "head").astype(jnp.float32)
    share_width = partial_value.shape[1] // lax.axis_size("head")
    projected = lax.dynamic_slice_in_dim(
        summed, lax.axis_index("head") * share_width, share_width, 1
    )
    return (projected.astype(jnp.bfloat16), keys_updated, values_updated)


def solution(mesh):
    return jax.shard_map(
        shards,
        mesh=mesh,
        in_specs=(
            P("seq", "head"),
            P(),
            P(None, "head"),
            P(None, "head"),
            P(None, "head"),
            P("head", None),
            P("seq", "head"),
            P("seq", "head"),
            P(),
            P(),
        ),
        out_specs=(P("seq", "head"), P("seq", "head"), P("seq", "head")),
        check_vma=False,
    )
```

profile of v0, /device:TPU:1, one launch (start us, length us, event | category | flops | bytes accessed | tf_op | source)
XLA Modules:
  0.0 638.6 jit_solution(14705658243390205139)
XLA Ops:
  17.2 24.9 %all-gather.2.cloned.1.call-done = bf16[256,3072]{1,0:T(8,128)(2,1)} async-done(((bf16[256,384]{1,0:T(8,128)(2,1)}), bf16[256,3072]{1,0:T(8,128)(2,1)}) %all-gather.2.cloned.1.call-update) | async-done | bytes 1572880 | tf_op jit(solution)/shard_map/all_gather | solution.py:49
  44.5 2.4 convolution_bitcast_fusion.1
  47.4 2.3 convolution_convert_fusion.1
  50.8 3.2 scatter_custom_fusion.2
  55.1 3.2 scatter_custom_fusion.3
  58.3 3.3 fusion.81
  72.7 386.6 %while.25 = (s32[]{:T(128)}, bf16[2,2304,128]{2,1,0:T(8,128)(2,1)}, f32[1,768]{1,0:T(1,128)S(1)}, f32[1,768]{1,0:T(1,128)}, f32[1,768,128]{2,1,0:T(8,128)}, /*in...) while((s32[]{:T(128)}, bf16[2,2304,128]{2,1,0:T(8,128)(2,1)}, ...), condition=%wide.region_14.15_spmd, body=%wide.region_7.14_spmd.sunk | while | flops 929181184 | bytes 57951692 | solution.py:184
  72.7 5.5 collective-permute-start
  80.0 40.8 %collective-permute-done = bf16[2,2304,128]{2,1,0:T(8,128)(2,1)S(1)} collective-permute-done((bf16[2,2304,128]{2,1,0:T(8,128)(2,1)}, bf16[2,2304,128]{2,1,0:T(8,128)(2,1)S(1)}, u32[]{:S(2)}, u32[]{:S(2)}) %collective-permute-start) | collective-permute-done | bytes 1179680 | tf_op jit(solution)/shard_map/while/body/eval_jaxpr/ppermute | solution.py:17
  120.8 2.1 fusion.105
  129.5 3.2 scatter_custom_fusion.14
  132.7 3.2 scatter_custom_fusion.15
  135.9 5.2 fusion.109
  141.1 2.9 collective-permute-start
  145.9 20.4 %collective-permute-done = bf16[2,2304,128]{2,1,0:T(8,128)(2,1)S(1)} collective-permute-done((bf16[2,2304,128]{2,1,0:T(8,128)(2,1)}, bf16[2,2304,128]{2,1,0:T(8,128)(2,1)S(1)}, u32[]{:S(2)}, u32[]{:S(2)}) %collective-permute-start) | collective-permute-done | bytes 1179680 | tf_op jit(solution)/shard_map/while/body/eval_jaxpr/ppermute | solution.py:17
  166.3 2.1 fusion.105
  175.1 3.2 scatter_custom_fusion.14
  178.3 3.2 scatter_custom_fusion.15
  181.5 5.2 fusion.109
  186.7 6.0 collective-permute-start
  194.5 33.1 %collective-permute-done = bf16[2,2304,128]{2,1,0:T(8,128)(2,1)S(1)} collective-permute-done((bf16[2,2304,128]{2,1,0:T(8,128)(2,1)}, bf16[2,2304,128]{2,1,0:T(8,128)(2,1)S(1)}, u32[]{:S(2)}, u32[]{:S(2)}) %collective-permute-start) | collective-permute-done | bytes 1179680 | tf_op jit(solution)/shard_map/while/body/eval_jaxpr/ppermute | solution.py:17
  227.7 2.1 fusion.105
  236.5 3.2 scatter_custom_fusion.14
  239.7 3.2 scatter_custom_fusion.15
  242.8 5.2 fusion.109
  249.9 29.8 %collective-permute-done = bf16[2,2304,128]{2,1,0:T(8,128)(2,1)S(1)} collective-permute-done((bf16[2,2304,128]{2,1,0:T(8,128)(2,1)}, bf16[2,2304,128]{2,1,0:T(8,128)(2,1)S(1)}, u32[]{:S(2)}, u32[]{:S(2)}) %collective-permute-start) | collective-permute-done | bytes 1179680 | tf_op jit(solution)/shard_map/while/body/eval_jaxpr/ppermute | solution.py:17
  279.7 2.1 fusion.105
  288.4 3.2 scatter_custom_fusion.14
  291.6 3.2 scatter_custom_fusion.15
  294.8 5.2 fusion.109
  300.0 2.1 collective-permute-start
  304.0 29.9 %collective-permute-done = bf16[2,2304,128]{2,1,0:T(8,128)(2,1)S(1)} collective-permute-done((bf16[2,2304,128]{2,1,0:T(8,128)(2,1)}, bf16[2,2304,128]{2,1,0:T(8,128)(2,1)S(1)}, u32[]{:S(2)}, u32[]{:S(2)}) %collective-permute-start) | collective-permute-done | bytes 1179680 | tf_op jit(solution)/shard_map/while/body/eval_jaxpr/ppermute | solution.py:17
  333.8 2.1 fusion.105
  342.6 3.2 scatter_custom_fusion.14
  345.8 3.2 scatter_custom_fusion.15
  349.0 5.2 fusion.109
  357.3 30.0 %collective-permute-done = bf16[2,2304,128]{2,1,0:T(8,128)(2,1)S(1)} collective-permute-done((bf16[2,2304,128]{2,1,0:T(8,128)(2,1)}, bf16[2,2304,128]{2,1,0:T(8,128)(2,1)S(1)}, u32[]{:S(2)}, u32[]{:S(2)}) %collective-permute-start) | collective-permute-done | bytes 1179680 | tf_op jit(solution)/shard_map/while/body/eval_jaxpr/ppermute | solution.py:17
  387.4 2.1 fusion.105
  396.2 3.2 scatter_custom_fusion.14
  399.4 3.2 scatter_custom_fusion.15
  402.5 5.2 fusion.109
  409.6 29.4 %collective-permute-done = bf16[2,2304,128]{2,1,0:T(8,128)(2,1)S(1)} collective-permute-done((bf16[2,2304,128]{2,1,0:T(8,128)(2,1)}, bf16[2,2304,128]{2,1,0:T(8,128)(2,1)S(1)}, u32[]{:S(2)}, u32[]{:S(2)}) %collective-permute-start) | collective-permute-done | bytes 1179680 | tf_op jit(solution)/shard_map/while/body/eval_jaxpr/ppermute | solution.py:17
  439.0 2.1 fusion.105
  447.8 3.2 scatter_custom_fusion.14
  451.0 3.2 scatter_custom_fusion.15
  454.1 5.2 fusion.109
  461.3 2.2 convolution_convert_fusion
  463.5 166.7 %all-reduce.2.cloned.1.call-done = bf16[256,3072]{1,0:T(8,128)(2,1)} async-done(((bf16[256,3072]{1,0:T(8,128)(2,1)}), bf16[256,3072]{1,0:T(8,128)(2,1)}) %all-reduce.2.cloned.1.call-update) | async-done | bytes 1572880 | tf_op jit(solution)/shard_map/psum | solution.py:195
  (195 shorter events, 89.3 us)
Async XLA Ops:
  7.2 454.2 %copy-start = (bf16[384,3072]{1,0:T(8,128)(2,1)S(1)}, bf16[384,3072]{1,0:T(8,128)(2,1)}, u32[]{:S(2)}) copy-start(bf16[384,3072]{1,0:T(8,128)(2,1)} %param.17) | copy-start | bytes 7077892
  7.2 37.3 %copy-start.9 = (f32[3072]{0:T(1024)S(1)}, f32[3072]{0:T(1024)}, u32[]{:S(2)}) copy-start(f32[3072]{0:T(1024)} %param.13) | copy-start | bytes 36868
  7.2 34.9 %all-gather.2.cloned.1.call-start = ((), (), s32[]{:S(2)}) async-start(), calls=%async_computation | async-start | bytes 1769472 | tf_op jit(solution)/shard_map/all_gather | solution.py:49
  8.4 38.9 %copy-start.2 = (bf16[2048,128]{1,0:T(8,128)(2,1)}, bf16[2048,128]{1,0:T(8,128)(2,1)S(1)}, u32[]{:S(2)}) copy-start(bf16[2048,128]{1,0:T(8,128)(2,1)S(1)} %copy.52) | copy-start | bytes 1572868
  10.5 619.7 %all-reduce.2.cloned.1.call-start = ((), (), s32[]{:S(2)}) async-start(), calls=%async_computation.1 | async-start | bytes 3145728 | tf_op jit(solution)/shard_map/psum | solution.py:195
  43.9 0.6 copy-start.7
  49.7 8.6 %copy-start.8 = (f32[256]{0:T(256)S(1)}, f32[256]{0:T(256)}, u32[]{:S(2)}) copy-start(f32[256]{0:T(256)} %copy-done.7) | copy-start | bytes 3076
  58.3 3.4 copy-start.3
  58.3 3.4 copy-start.4
  72.7 48.1 %collective-permute-start = (bf16[2,2304,128]{2,1,0:T(8,128)(2,1)}, bf16[2,2304,128]{2,1,0:T(8,128)(2,1)S(1)}, u32[]{:S(2)}, u32[]{:S(2)}) collective-permute-start(bf16[2,2304,128]{2,1,0:T(8,128)(2,1)} %get-tuple-element.428), channel_id=1, source_target_pairs={{0,32},{8,40},{16,48},{24,56},{32,64},{40,72},{48,80},{56,88},{64,... | collective-permute-start | bytes 3538952 | tf_op jit(solution)/shard_map/while/body/eval_jaxpr/ppermute | solution.py:17
  122.8 4.2 copy-start.1
  125.5 1.8 copy-start.5
  127.3 1.2 copy-start.6
  141.1 25.3 %collective-permute-start = (bf16[2,2304,128]{2,1,0:T(8,128)(2,1)}, bf16[2,2304,128]{2,1,0:T(8,128)(2,1)S(1)}, u32[]{:S(2)}, u32[]{:S(2)}) collective-permute-start(bf16[2,2304,128]{2,1,0:T(8,128)(2,1)} %get-tuple-element.428), channel_id=1, source_target_pairs={{0,32},{8,40},{16,48},{24,56},{32,64},{40,72},{48,80},{56,88},{64,... | collective-permute-start | bytes 3538952 | tf_op jit(solution)/shard_map/while/body/eval_jaxpr/ppermute | solution.py:17
  168.4 4.2 copy-start.1
  171.1 1.8 copy-start.5
  172.9 1.2 copy-start.6
  186.7 41.0 %collective-permute-start = (bf16[2,2304,128]{2,1,0:T(8,128)(2,1)}, bf16[2,2304,128]{2,1,0:T(8,128)(2,1)S(1)}, u32[]{:S(2)}, u32[]{:S(2)}) collective-permute-start(bf16[2,2304,128]{2,1,0:T(8,128)(2,1)} %get-tuple-element.428), channel_id=1, source_target_pairs={{0,32},{8,40},{16,48},{24,56},{32,64},{40,72},{48,80},{56,88},{64,... | collective-permute-start | bytes 3538952 | tf_op jit(solution)/shard_map/while/body/eval_jaxpr/ppermute | solution.py:17
  229.8 4.2 copy-start.1
  232.4 1.8 copy-start.5
  234.3 1.2 copy-start.6
  248.0 31.7 %collective-permute-start = (bf16[2,2304,128]{2,1,0:T(8,128)(2,1)}, bf16[2,2304,128]{2,1,0:T(8,128)(2,1)S(1)}, u32[]{:S(2)}, u32[]{:S(2)}) collective-permute-start(bf16[2,2304,128]{2,1,0:T(8,128)(2,1)} %get-tuple-element.428), channel_id=1, source_target_pairs={{0,32},{8,40},{16,48},{24,56},{32,64},{40,72},{48,80},{56,88},{64,... | collective-permute-start | bytes 3538952 | tf_op jit(solution)/shard_map/while/body/eval_jaxpr/ppermute | solution.py:17
  281.8 4.2 copy-start.1
  284.4 1.8 copy-start.5
  286.2 1.2 copy-start.6
  300.0 33.9 %collective-permute-start = (bf16[2,2304,128]{2,1,0:T(8,128)(2,1)}, bf16[2,2304,128]{2,1,0:T(8,128)(2,1)S(1)}, u32[]{:S(2)}, u32[]{:S(2)}) collective-permute-start(bf16[2,2304,128]{2,1,0:T(8,128)(2,1)} %get-tuple-element.428), channel_id=1, source_target_pairs={{0,32},{8,40},{16,48},{24,56},{32,64},{40,72},{48,80},{56,88},{64,... | collective-permute-start | bytes 3538952 | tf_op jit(solution)/shard_map/while/body/eval_jaxpr/ppermute | solution.py:17
  335.9 4.2 copy-start.1
  338.6 1.8 copy-start.5
  340.4 1.2 copy-start.6
  354.2 33.2 %collective-permute-start = (bf16[2,2304,128]{2,1,0:T(8,128)(2,1)}, bf16[2,2304,128]{2,1,0:T(8,128)(2,1)S(1)}, u32[]{:S(2)}, u32[]{:S(2)}) collective-permute-start(bf16[2,2304,128]{2,1,0:T(8,128)(2,1)} %get-tuple-element.428), channel_id=1, source_target_pairs={{0,32},{8,40},{16,48},{24,56},{32,64},{40,72},{48,80},{56,88},{64,... | collective-permute-start | bytes 3538952 | tf_op jit(solution)/shard_map/while/body/eval_jaxpr/ppermute | solution.py:17
  389.5 4.2 copy-start.1
  392.1 1.8 copy-start.5
  394.0 1.2 copy-start.6
  407.7 31.3 %collective-permute-start = (bf16[2,2304,128]{2,1,0:T(8,128)(2,1)}, bf16[2,2304,128]{2,1,0:T(8,128)(2,1)S(1)}, u32[]{:S(2)}, u32[]{:S(2)}) collective-permute-start(bf16[2,2304,128]{2,1,0:T(8,128)(2,1)} %get-tuple-element.428), channel_id=1, source_target_pairs={{0,32},{8,40},{16,48},{24,56},{32,64},{40,72},{48,80},{56,88},{64,... | collective-permute-start | bytes 3538952 | tf_op jit(solution)/shard_map/while/body/eval_jaxpr/ppermute | solution.py:17
  441.1 4.2 copy-start.1
  443.7 1.8 copy-start.5
  445.6 1.2 copy-start.6
Sparse Core Ops, SparseCore 0:
  10.6 31.4 all-gather.1
  463.6 166.5 all-reduce.1
where the time goes:
time: 642 us; the launch traced here: 639 us
  waiting for transfers between devices  405 us (63%)
  matrix products  84.8 us (13%)
  local copies, waits for them, and re-layouts  67 us (10%)
  other arithmetic  48 us (7%)
  starting transfers between devices  17.9 us (3%)
  between operations  15.5 us (2%)
    ppermute x7, waiting for transfers between devices, shifted(): lax.ppermute(shard, axis, [(i, (i + by) % devices) for i in range(devices)])  213 us
    psum x1, waiting for transfers between devices, shards(): lax.psum(partial_value.astype(jnp.bfloat16), 'head').astype(jnp.float32)  167 us
    dot_general x16, matrix products, attend(): jnp.einsum('gqk,kgd->gqd', weights.astype(jnp.bfloat16), value_block.resh...  46.8 us
    dot_general x16, matrix products, attend(): jnp.einsum('gqd,kgd->gqk', query_group, key_block.reshape(-1, kv_heads, H...  27.9 us
    scatter x8, local copies, waits for them, and re-layouts, write_fresh(): out_keys = out_keys.at[target].set(fresh_keys, mode='drop')  25.5 us
    scatter x8, local copies, waits for them, and re-layouts, write_fresh(): out_values = out_values.at[target].set(fresh_values, mode='drop')  25.5 us
    all_gather x1, waiting for transfers between devices, shards(): gathered = lax.all_gather(tokens, 'head', axis=1, tiled=True)  24.9 us
    ppermute x7, starting transfers between devices, shifted(): lax.ppermute(shard, axis, [(i, (i + by) % devices) for i in range(devices)])  17.8 us
  transfers between devices with their start and end apart: 9, of which 9 were waited for; matrix products, arithmetic and copies ran while one was open for 3% of the time, Pallas kernels for 0%

commit v1 on v0

v1 whole, which is shorter than its diff:
```python
import math

import jax
import jax.numpy as jnp
from jax import lax
from jax.experimental import pallas as pl
from jax.experimental.pallas import tpu as pltpu
from jax.sharding import PartitionSpec as P

HD = 128
NX = 4
NZ = 8
NY = 4
GROUP = 8
NEG = -(2.0**100)
ROPE_BASE = 500000.0
EPS = 1e-05
LOG2E = 1.4426950408889634
F32 = jnp.float32
BF16 = jnp.bfloat16


def digit(number, place):
    value = number
    result = value % 10
    for at in range(1, 8):
        value = value // 10
        flag = (place + 8 - at) // 8 - (place + 7 - at) // 8
        result = result + flag * (value % 10 - number % 10)
    return result


def order_code(digits):
    return sum(d * 10**i for i, d in enumerate(digits))


ORDER = [(0, 0), (0, 1), (0, 3), (1, 0), (0, 2), (1, 1), (1, 3), (1, 2)]
STEP_FORWARD_Q = ORDER.index((1, 0))
STEP_SEND_KV = 1
STEP_FORWARD_KV = 6


def kernel(
    tok, gain, wq, wk, wv, wo, kc, vc, lens, cos, sin,
    out, kv_out,
    x_all, wq_v, wk_v, wv_v, wo_all, kraw, kT, va, kfT, vfa, acc, ssq,
    q_all, kv_all, o_buf, l_buf, o_in, l_in, oz_out, lz_out, oz_in, lz_in,
    att_all, pr_out, pr_in,
    load_sem, own_wo_sem, ag_send, ag_recv, wo_send, wo_recv, q_send, q_recv, kv_send, kv_recv,
    o_send, o_recv, l_send, l_recv, z_send, z_recv, att_send, att_recv, pr_send, pr_recv, out_sem,
):
    rows, width = tok.shape
    heads = width // HD
    slots = kc.shape[0]
    s = lax.axis_index("seq")
    h = lax.axis_index("head")
    x, z = s // NZ, s % NZ
    zhi = z // 4
    request = s % 4
    y, c = h // 2, h % 2
    p = s // 4
    z_peer = x * NZ + (z + 4) % NZ
    pz = z_peer // 4
    sib = y * 2 + (1 - c)

    def x_peer(d):
        return ((x + d) % NX) * NZ + z

    def y_peer(d):
        return ((y + d) % NY) * 2 + c

    def remote(src, dst, send, recv, seq, head):
        return pltpu.make_async_remote_copy(
            src_ref=src, dst_ref=dst, send_sem=send, recv_sem=recv,
            device_id=(seq, head), device_id_type=pl.DeviceIdType.MESH,
        )

    loads = [
        pltpu.make_async_copy(tok, x_all.at[h], load_sem.at[0]),
        pltpu.make_async_copy(wq, wq_v, load_sem.at[1]),
        pltpu.make_async_copy(wk, wk_v, load_sem.at[2]),
        pltpu.make_async_copy(wv, wv_v, load_sem.at[3]),
        pltpu.make_async_copy(kc, kraw, load_sem.at[4]),
        pltpu.make_async_copy(vc, va.at[:, pl.ds(0, HD)], load_sem.at[5]),
    ]
    for load in loads:
        load.start()

    def wo_columns(yy, cc):
        return wo.at[:, pl.ds(pl.multiple_of((yy * 2 + cc) * width, width), width)]

    def wo_rows(yy, cc):
        return wo_all.at[yy, pl.ds(pl.multiple_of(cc * width, width), width), :]

    own_wo = [
        pltpu.make_async_copy(wo_columns(yy, c), wo_rows(yy, c), own_wo_sem.at[yy])
        for yy in range(NY)
    ]
    for load in own_wo:
        load.start()

    barrier = pltpu.get_barrier_semaphore()
    peers = [(s, sib), (z_peer, h)]
    peers += [(s, y_peer(d)) for d in (1, 2, 3)] + [(x_peer(d), h) for d in (1, 2, 3)]
    for seq, head in peers:
        pl.semaphore_signal(
            barrier, inc=1, device_id=(seq, head), device_id_type=pl.DeviceIdType.MESH
        )
    pl.semaphore_wait(barrier, len(peers))

    def ag_copy(k, source, seq, head, src=None):
        return remote(
            x_all.at[source] if src is None else src, x_all.at[source],
            ag_send.at[k], ag_recv.at[source], seq, head,
        )

    for k, d in enumerate((2, 1, 3)):
        ag_copy(k, h, s, y_peer(d), tok).start()
    ag_copy(3, h, s, sib, tok).start()
    wo_copies = [
        remote(wo_columns(yy, 1 - c), wo_rows(yy, c), wo_send.at[yy], wo_recv.at[yy], s, sib)
        for yy in range(NY)
    ]
    for copy in wo_copies:
        copy.start()

    length = lens[request]
    loads[4].wait()
    loads[5].wait()
    for at in range(0, slots, 512):
        kT[pl.ds(0, HD), pl.ds(at, 512)] = kraw[pl.ds(at, 512), :].T
    slot = p * slots + lax.broadcasted_iota(jnp.int32, (HD, slots), 1)
    first_row = lax.broadcasted_iota(jnp.int32, (HD, slots), 0) == 0
    hidden = jnp.logical_and(first_row, slot >= length)
    kT[pl.ds(HD, HD), :] = jnp.where(hidden, NEG, 0.0).astype(BF16)
    va[:, pl.ds(HD, HD)] = jnp.ones((slots, HD), BF16)
    vfa[:, pl.ds(HD, HD)] = jnp.ones((rows, HD), BF16)
    acc[...] = jnp.zeros_like(acc)
    ssq[...] = jnp.zeros_like(ssq)

    for at in range(4):
        loads[at].wait()

    def project(step, unused):
        d = digit(order_code([0, 0, 1, 3, 2, 1, 3, 2]), step)
        other = digit(order_code([0, 1, 0, 0, 0, 1, 1, 1]), step)
        source = ((y + d) % NY) * 2 + (c + other) % 2

        @pl.when(step > 0)
        def _():
            ag_copy(0, source, s, sib).wait_recv()

        @pl.when(jnp.logical_and(step >= 2, step < 5))
        def _():
            ag_copy(2 + step, source, s, sib).start()

        shard = x_all[source].astype(F32)
        square = shard * shard
        ssq[...] += square[:, :HD] + square[:, HD:2 * HD] + square[:, 2 * HD:]
        scaled = (shard * gain[source]).astype(BF16)
        at = pl.ds(pl.multiple_of(source * width, width), width)
        acc[:, pl.ds(0, width)] += jnp.dot(scaled, wq_v[at, :], preferred_element_type=F32)
        acc[:, pl.ds(width, HD)] += jnp.dot(scaled, wk_v[at, :], preferred_element_type=F32)
        acc[:, pl.ds(width + HD, HD)] += jnp.dot(scaled, wv_v[at, :], preferred_element_type=F32)
        return unused

    lax.fori_loop(0, 8, project, 0)

    scale = lax.rsqrt(jnp.sum(ssq[...], -1, keepdims=True) * (1.0 / (width * 8)) + EPS)
    cosine = cos[...]
    sine = sin[...]

    def rope(vectors):
        return vectors * cosine + pltpu.roll(vectors, HD // 2, 1) * sine

    fold = LOG2E / math.sqrt(HD)
    for hd in range(heads):
        rotated = rope(acc[:, pl.ds(hd * HD, HD)] * scale) * fold
        q_all[p, pl.ds(hd * rows, rows), :] = rotated.astype(BF16)

    def q_copy(k, block, seq):
        return remote(
            q_all.at[block], q_all.at[block], q_send.at[k], q_recv.at[block], seq, h
        )

    def kv_copy(k, block, seq):
        return remote(
            kv_all.at[:, block], kv_all.at[:, block], kv_send.at[k], kv_recv.at[block], seq, h
        )

    q_copy(0, p, z_peer).start()
    for k, d in enumerate((1, 3, 2)):
        q_copy(1 + k, p, x_peer(d)).start()

    fresh_key = rope(acc[:, pl.ds(width, HD)] * scale).astype(BF16)
    fresh_value = (acc[:, pl.ds(width + HD, HD)] * scale).astype(BF16)
    kv_all[0, p] = fresh_key
    kv_all[1, p] = fresh_value
    kfT[...] = fresh_key.T
    vfa[:, pl.ds(0, HD)] = fresh_value

    eye = lax.broadcasted_iota(jnp.int32, (HD, HD), 0) == lax.broadcasted_iota(
        jnp.int32, (HD, HD), 1
    )
    first_lane = lax.broadcasted_iota(jnp.int32, (rows, HD), 1) == 0
    one_lane = jnp.where(first_lane, 1.0, 0.0).astype(BF16)
    offset = lax.broadcasted_iota(jnp.int32, (rows, rows), 0) - lax.broadcasted_iota(
        jnp.int32, (rows, rows), 1
    )

    def o_copies(dz, dx):
        back = (NX - dx) % NX
        return (
            remote(o_buf.at[dz, dx], o_in.at[dz, back], o_send.at[dz, dx], o_recv.at[dz, back],
                   x_peer(dx), h),
            remote(l_buf.at[dz, dx], l_in.at[dz, back], l_send.at[dz, dx], l_recv.at[dz, back],
                   x_peer(dx), h),
        )

    def attend(step, unused):
        dz = digit(order_code([o[0] for o in ORDER]), step)
        dx = digit(order_code([o[1] for o in ORDER]), step)
        block = 2 * ((x + dx) % NX) + (zhi + dz) % 2

        @pl.when(dx + dz > 0)
        def _():
            q_copy(0, block, z_peer).wait_recv()

        @pl.when(step == STEP_FORWARD_Q)
        def _():
            for k, d in enumerate((1, 3, 2)):
                q_copy(4 + k, pz, x_peer(d)).start()

        @pl.when(step == STEP_SEND_KV)
        def _():
            kv_copy(0, p, z_peer).start()
            for k, d in enumerate((1, 3, 2)):
                kv_copy(1 + k, p, x_peer(d)).start()

        @pl.when(step == STEP_FORWARD_KV)
        def _():
            kv_copy(0, pz, z_peer).wait_recv()
            for k, d in enumerate((1, 3, 2)):
                kv_copy(4 + k, pz, x_peer(d)).start()

        def one_head(hd, inner):
            at = pl.ds(pl.multiple_of(hd * rows, rows), rows)
            query = q_all[block, at, :]
            cached = jnp.dot(
                jnp.concatenate([query, one_lane], 1), kT[...], preferred_element_type=F32
            )
            fresh = jnp.dot(query, kfT[...], preferred_element_type=F32)
            fresh = jnp.where(offset + (block - p) * rows >= 0, fresh, NEG)
            top = jnp.maximum(
                jnp.max(cached, -1, keepdims=True), jnp.max(fresh, -1, keepdims=True)
            )
            cached_weights = jnp.exp2(cached - top).astype(BF16)
            fresh_weights = jnp.exp2(fresh - top).astype(BF16)
            summed = jnp.dot(cached_weights, va[...], preferred_element_type=F32)
            summed += jnp.dot(fresh_weights, vfa[...], preferred_element_type=F32)
            total = summed[:, HD:]
            o_buf[dz, dx, at, :] = (summed[:, :HD] / total).astype(BF16)
            logsum = top + jnp.log(total) * LOG2E
            for half in range(rows // HD):
                part = logsum[half * HD:(half + 1) * HD, :]
                l_buf[dz, dx, hd, pl.ds(half, 1), :] = jnp.sum(
                    jnp.where(eye, part, 0.0), 0, keepdims=True
                )
            return inner

        lax.fori_loop(0, heads, one_head, 0)

        @pl.when(dx > 0)
        def _():
            for copy in o_copies(dz, dx):
                copy.start()

        return unused

    l_buf[...] = jnp.zeros_like(l_buf)
    lax.fori_loop(0, GROUP, attend, 0)

    def weigh(logsums):
        highest = logsums[0]
        for one in logsums[1:]:
            highest = jnp.maximum(highest, one)
        shares = [jnp.exp2(one - highest) for one in logsums]
        total = shares[0]
        for one in shares[1:]:
            total = total + one
        return [one / total for one in shares], highest + jnp.log(total) * LOG2E

    def blend(parts, shares, hd, half):
        result = None
        for part, share in zip(parts, shares):
            lanes = share[hd, half:half + 1, :]
            column = jnp.sum(jnp.where(eye, lanes, 0.0), 1, keepdims=True)
            window = pl.ds(hd * rows + half * HD, HD)
            term = part[window, :].astype(F32) * column
            result = term if result is None else result + term
        return result

    def contributions(dz):
        for j in (1, 3, 2):
            for copy in o_copies(dz, (NX - j) % NX):
                copy.wait_recv()
        parts = [o_buf.at[dz, 0]] + [o_in.at[dz, j] for j in (1, 2, 3)]
        logsums = [l_buf[dz, 0]] + [l_in[dz, j] for j in (1, 2, 3)]
        return parts, logsums

    z_copies = (
        remote(oz_out, oz_in, z_send.at[0], z_recv.at[0], z_peer, h),
        remote(lz_out, lz_in, z_send.at[1], z_recv.at[1], z_peer, h),
    )
    parts, logsums = contributions(1)
    shares, merged = weigh(logsums)
    lz_out[...] = merged
    for hd in range(heads):
        for half in range(rows // HD):
            oz_out[pl.ds(hd * rows + half * HD, HD), :] = blend(parts, shares, hd, half).astype(BF16)
    for copy in z_copies:
        copy.start()

    for d in (1, 2, 3):
        kv_copy(0, 2 * ((x + d) % NX) + zhi, z_peer).wait_recv()
        kv_copy(0, 2 * ((x + d) % NX) + (zhi + 1) % 2, z_peer).wait_recv()
    kv_store = pltpu.make_async_copy(kv_all, kv_out.at[:, pl.ds(GROUP, GROUP)], out_sem)
    kv_store.start()

    parts, logsums = contributions(0)
    for copy in z_copies:
        copy.wait_recv()
    shares, merged = weigh(logsums + [lz_in[...]])
    for hd in range(heads):
        for half in range(rows // HD):
            att_all[c, pl.ds(half * HD, HD), pl.ds(hd * HD, HD)] = blend(
                parts + [oz_in], shares, hd, half
            ).astype(BF16)
    att_copy = remote(att_all.at[c], att_all.at[c], att_send, att_recv, s, sib)
    att_copy.start()
    for load in own_wo:
        load.wait()
    for copy in wo_copies:
        copy.wait_recv()
    remote(att_all.at[1 - c], att_all.at[1 - c], att_send, att_recv, s, sib).wait_recv()
    both = jnp.concatenate([att_all[0], att_all[1]], 1)

    def pr_copy(d):
        return remote(
            pr_out.at[d], pr_in.at[(NY - d) % NY], pr_send.at[d], pr_recv.at[(NY - d) % NY],
            s, y_peer(d),
        )

    for d in (2, 1, 3):
        part = jnp.dot(both, wo_all[(y + d) % NY], preferred_element_type=F32)
        pr_out[d] = part.astype(BF16)
        pr_copy(d).start()
    result = jnp.dot(both, wo_all[y], preferred_element_type=F32)
    for j in (1, 3, 2):
        pr_copy((NY - j) % NY).wait_recv()
    for j in (1, 2, 3):
        result = result + pr_in[j].astype(F32)
    out[...] = result.astype(BF16)

    for k in range(3):
        ag_copy(k, h, s, sib, tok).wait_send()
    ag_copy(3, h, s, sib, tok).wait_send()
    for k in range(4, 7):
        ag_copy(k, h, s, sib).wait_send()
    for copy in wo_copies:
        copy.wait_send()
    for k in range(7):
        q_copy(k, p, z_peer).wait_send()
        kv_copy(k, p, z_peer).wait_send()
    for dz in range(2):
        for dx in (1, 2, 3):
            for copy in o_copies(dz, dx):
                copy.wait_send()
    for copy in z_copies:
        copy.wait_send()
    att_copy.wait_send()
    for d in (1, 2, 3):
        pr_copy(d).wait_send()
    kv_store.wait()


def shards(
    tokens, norm_gain, w_query, w_key, w_value, w_out, keys_cache, values_cache,
    cached_lengths, rope_offsets,
):
    rows, width = tokens.shape
    slots = keys_cache.shape[0]
    heads = width // HD
    member = lax.axis_index("seq")
    request = member % 4
    place = member // 4
    length = lax.dynamic_index_in_dim(cached_lengths, request, 0, False)
    offset = lax.dynamic_index_in_dim(rope_offsets, request, 0, False)
    positions = offset + length + place * rows + jnp.arange(rows, dtype=jnp.int32)
    frequency = ROPE_BASE ** (-jnp.arange(HD // 2, dtype=F32) * 2.0 / HD)
    angles = positions.astype(F32)[:, None] * frequency[None, :]
    cosine = jnp.cos(angles)
    sine = jnp.sin(angles)
    cosine = jnp.concatenate([cosine, cosine], 1)
    sine = jnp.concatenate([-sine, sine], 1)

    any_spec = pl.BlockSpec(memory_space=pl.ANY)
    vmem_spec = pl.BlockSpec(memory_space=pltpu.VMEM)
    smem_spec = pl.BlockSpec(memory_space=pltpu.SMEM)
    dma = pltpu.SemaphoreType.DMA
    block = (heads * rows, HD)
    projected, fresh = pl.pallas_call(
        kernel,
        out_shape=(
            jax.ShapeDtypeStruct((rows, width), BF16),
            jax.ShapeDtypeStruct((2, 3 * GROUP, rows, HD), BF16),
        ),
        in_specs=[any_spec, vmem_spec] + [any_spec] * 6 + [smem_spec, vmem_spec, vmem_spec],
        out_specs=(vmem_spec, any_spec),
        scratch_shapes=[
            pltpu.VMEM((8, rows, width), BF16),
            pltpu.VMEM(w_query.shape, BF16),
            pltpu.VMEM(w_key.shape, BF16),
            pltpu.VMEM(w_value.shape, BF16),
            pltpu.VMEM((NY, 2 * width, width), BF16),
            pltpu.VMEM((slots, HD), BF16),
            pltpu.VMEM((2 * HD, slots), BF16),
            pltpu.VMEM((slots, 2 * HD), BF16),
            pltpu.VMEM((HD, rows), BF16),
            pltpu.VMEM((rows, 2 * HD), BF16),
            pltpu.VMEM((rows, width + 2 * HD), F32),
            pltpu.VMEM((rows, HD), F32),
            pltpu.VMEM((GROUP,) + block, BF16),
            pltpu.VMEM((2, GROUP, rows, HD), BF16),
            pltpu.VMEM((2, NX) + block, BF16),
            pltpu.VMEM((2, NX, heads, 8, HD), F32),
            pltpu.VMEM((2, NX) + block, BF16),
            pltpu.VMEM((2, NX, heads, 8, HD), F32),
            pltpu.VMEM(block, BF16),
            pltpu.VMEM((heads, 8, HD), F32),
            pltpu.VMEM(block, BF16),
            pltpu.VMEM((heads, 8, HD), F32),
            pltpu.VMEM((2, rows, width), BF16),
            pltpu.VMEM((NY, rows, width), BF16),
            pltpu.VMEM((NY, rows, width), BF16),
            dma((6,)), dma((NY,)), dma((7,)), dma((8,)), dma((NY,)), dma((NY,)),
            dma((7,)), dma((GROUP,)), dma((7,)), dma((GROUP,)),
            dma((2, NX)), dma((2, NX)), dma((2, NX)), dma((2, NX)),
            dma((2,)), dma((2,)), dma, dma, dma((NY,)), dma((NY,)), dma,
        ],
        compiler_params=pltpu.CompilerParams(
            collective_id=0, has_side_effects=True, vmem_limit_bytes=48 << 20
        ),
        name="span_attention",
    )(
        tokens, norm_gain.reshape(8, 1, width), w_query, w_key, w_value, w_out,
        keys_cache, values_cache, cached_lengths, cosine, sine,
    )
    fresh = fresh.reshape(2, 3 * GROUP * rows, HD)
    start = place * slots - length
    token = start + jnp.arange(slots, dtype=jnp.int32)
    written = jnp.logical_and(token >= 0, token < GROUP * rows)[:, None]
    begin = jnp.clip(start + GROUP * rows, 0, 2 * GROUP * rows)

    def update(at, cache):
        window = lax.dynamic_slice(fresh, (at, begin, 0), (1, slots, HD))[0]
        return jnp.where(written, window, cache)

    return projected, update(0, keys_cache), update(1, values_cache)


def solution(mesh):
    return jax.shard_map(
        shards,
        mesh=mesh,
        in_specs=(
            P("seq", "head"), P(), P(None, "head"), P(None, "head"), P(None, "head"),
            P("head", None), P("seq", "head"), P("seq", "head"), P(), P(),
        ),
        out_specs=(P("seq", "head"), P("seq", "head"), P("seq", "head")),
        check_vma=False,
    )
```

time: 642 us -> 115 us (0.18)
  the two profiles are of different devices: /device:TPU:1 before, /device:TPU:35 now
where the time goes in v1:
time: 115 us
  Pallas kernels  97.3 us (85%)
  local copies, waits for them, and re-layouts  11.5 us (10%)
  other arithmetic  3.32 us (3%)
  between operations  2.67 us (2%)
    pallas_call x1, Pallas kernels, shards(): pl.pallas_call(kernel, out_shape=(jax.ShapeDtypeStruct((rows, width), BF1...  97.3 us
    unnamed x17, local copies, waits for them, and re-layouts  8.97 us
    select_n x1, other arithmetic, update(): return jnp.where(written, window, cache)  2.63 us

profile of v1, /device:TPU:35, one launch (start us, length us, event | category | flops | bytes accessed | tf_op | source)
XLA Modules:
  0.0 114.7 jit_solution(8410126774519213416)
XLA Ops:
  0.7 1.2 %dynamic_slice.14 = s32[1]{0:T(128)} dynamic-slice(s32[4]{0:T(128)} %lens.1, s32[]{:T(128)S(6)} %select_n.26), dynamic_slice_sizes={1} | dynamic-slice | bytes 12 | tf_op jit(solution)/shard_map/jit(dynamic_index_in_dim)/dynamic_slice | solution.py:397
  2.6 1.2 %dynamic_slice.13 = s32[1]{0:T(128)} dynamic-slice(s32[4]{0:T(128)} %param.19, s32[]{:T(128)S(6)} %select_n.26), dynamic_slice_sizes={1} | dynamic-slice | bytes 12 | tf_op jit(solution)/shard_map/jit(dynamic_index_in_dim)/dynamic_slice | solution.py:398
  5.1 0.5 fusion
  5.7 0.1 pad_maximum_fusion
  5.8 0.0 copy-start
  5.8 1.7 %copy-done = bf16[3072,384]{1,0:T(8,128)(2,1)S(1)} copy-done((bf16[3072,384]{1,0:T(8,128)(2,1)S(1)}, bf16[3072,384]{1,0:T(8,128)(2,1)}, u32[]{:S(2)}) %copy-start) | copy-done | bytes 2359320
  7.5 0.0 copy-start.1
  7.5 1.0 copy-done.1
  8.5 0.0 copy-start.2
  8.5 1.0 copy-done.2
  9.6 0.0 copy-start.3
  9.6 1.1 copy-done.3
  10.7 0.0 copy-start.4
  10.7 1.1 copy-done.4
  11.8 0.0 copy-start.5
  11.8 0.9 copy-done.5
  12.8 0.0 copy-start.6
  12.8 0.7 copy-done.6
  13.5 0.0 copy-start.7
  13.5 0.7 copy-done.7
  14.1 97.3 %span_attention.1 = (bf16[256,384]{1,0:T(8,128)(2,1)S(1)}, bf16[2,24,256,128]{3,2,1,0:T(8,128)(2,1)}) custom-call(bf16[256,384]{1,0:T(8,128)(2,1)S(1)} %copy-done.5, f32[8,1,384]{2,1,0:T(1,128)S(1)} %bitcast.8, bf16[3072,384]{1,0:T(8,128)(2,1)S(1)} %copy-done, bf16[3072,128]{1,0:T(8,128)(2,1)S(1)} %copy-done.3, bf16[3072,128]{1,0:T(8,128)(2,1)S(1)} %copy-done.4, ...), custom_call_target="tpu_custom_call" | custom-call | tf_op jit(solution)/shard_map/span_attention/pallas_call | solution.py:412
  111.4 2.6 %bitcast_select_fusion = (bf16[2048,128]{1,0:T(8,128)(2,1)}, bf16[2048,128]{1,0:T(8,128)(2,1)}) fusion(bf16[2048,128]{1,0:T(8,128)(2,1)S(1)} %copy-done.2, bf16[2,6144,128]{2,1,0:T(8,128)(2,1)} %bitcast.9, s32[]{:T(128)S(6)} %min.4, pred[2048]{0:T(1024)(128)(4,1)S(1)} %fusion.3, bf16[2048,128]{1,0:T(8,128)(2,1)S(1)} %copy-done.1), kind=kLoop, calls=%fused_computation | loop fusion | flops 524288 | bytes 3147780 | tf_op jit(solution)/shard_map/jit(_where)/select_n | solution.py:467
  114.1 0.7 copy.14
  (3 shorter events, 0.0 us)
Async XLA Ops:
  5.8 1.7 %copy-start = (bf16[3072,384]{1,0:T(8,128)(2,1)S(1)}, bf16[3072,384]{1,0:T(8,128)(2,1)}, u32[]{:S(2)}) copy-start(bf16[3072,384]{1,0:T(8,128)(2,1)} %wq.1) | copy-start | bytes 7077892
  7.5 1.0 copy-start.1
  8.5 1.0 copy-start.2
  9.6 1.1 copy-start.3
  10.7 1.1 copy-start.4
  11.8 0.9 copy-start.5
  12.8 0.7 copy-start.6
  13.5 0.7 copy-start.7

commit v2 on v1

v2 whole, which is shorter than its diff:
```python
import math

import jax
import jax.numpy as jnp
import numpy as np
from jax import lax
from jax.experimental import pallas as pl
from jax.experimental.pallas import tpu as pltpu
from jax.sharding import PartitionSpec as P

HD = 128
NX = 4
NZ = 8
NY = 4
GROUP = 8
NEG = -(2.0**100)
ROPE_BASE = 500000.0
EPS = 1e-05
LOG2E = 1.4426950408889634
F32 = jnp.float32
BF16 = jnp.bfloat16


def digit(number, place):
    value = number
    result = value % 10
    for at in range(1, 8):
        value = value // 10
        flag = (place + 8 - at) // 8 - (place + 7 - at) // 8
        result = result + flag * (value % 10 - number % 10)
    return result


def order_code(digits):
    return sum(d * 10**i for i, d in enumerate(digits))


ORDER = [(0, 0, 0), (0, 0, 1), (0, 1, 0), (1, 0, 0), (1, 1, 0), (1, 0, 1), (1, 1, 1), (0, 1, 1)]
STEP_FORWARD = (3, 5)
STEP_MERGE = 5
CHUNK = 1024
CHUNKS = 2


def kernel(
    tok, gain, wq, wk, wv, wo, kc, vc, freq, lens, offs,
    out, keys_out, values_out,
    x_all, gain_v, freq_v, wq_v, wk_v, wv_v, wo_all, kraw, kT, va, kfT, vfa, acc, ssq,
    cos, sin, fresh_pad, updated, q_all, kv_all, o_buf, l_buf, o_in, l_in,
    oz_out, lz_out, oz_in, lz_in, att_all, pr_out, pr_in, own_part,
    load_sem, own_wo_sem, ag_send, ag_recv, wo_send, wo_recv, pair_send, pair_recv,
    q_send, q_recv, kv_send, kv_recv, o_send, o_recv, l_send, l_recv,
    z_send, z_recv, lz_send, lz_recv, att_send, att_recv, pr_send, pr_recv, out_sem,
):
    rows, width = tok.shape
    heads = width // HD
    slots = kc.shape[0]
    s = lax.axis_index("seq")
    h = lax.axis_index("head")
    x, z = s // NZ, s % NZ
    zhi = z // 4
    request = s % 4
    y, c = h // 2, h % 2
    p = s // 4
    z_peer = x * NZ + (z + 4) % NZ
    pz = z_peer // 4
    sib = y * 2 + (1 - c)
    odd = (x + c) % 2
    to_pair, to_next = 1 + 2 * odd, 3 - 2 * odd
    px = 2 * ((x + to_pair) % NX) + zhi
    part_rows = rows // CHUNKS

    def x_peer(d):
        return ((x + d) % NX) * NZ + z

    def y_peer(d):
        return ((y + d) % NY) * 2 + c

    def remote(src, dst, send, recv, seq, head):
        return pltpu.make_async_remote_copy(
            src_ref=src, dst_ref=dst, send_sem=send, recv_sem=recv,
            device_id=(seq, head), device_id_type=pl.DeviceIdType.MESH,
        )

    loads = [
        pltpu.make_async_copy(tok, x_all.at[h], load_sem.at[0]),
        pltpu.make_async_copy(wq, wq_v, load_sem.at[1]),
        pltpu.make_async_copy(wk, wk_v, load_sem.at[2]),
        pltpu.make_async_copy(wv, wv_v, load_sem.at[3]),
        pltpu.make_async_copy(kc, kraw.at[0], load_sem.at[4]),
        pltpu.make_async_copy(vc, va.at[0, :, pl.ds(0, HD)], load_sem.at[5]),
        pltpu.make_async_copy(gain, gain_v, load_sem.at[6]),
        pltpu.make_async_copy(freq, freq_v, load_sem.at[7]),
    ]
    for load in loads:
        load.start()

    def wo_columns(yy, cc):
        return wo.at[:, pl.ds(pl.multiple_of((yy * 2 + cc) * width, width), width)]

    def wo_rows(yy, cc):
        return wo_all.at[yy, pl.ds(pl.multiple_of(cc * width, width), width), :]

    own_wo = [
        pltpu.make_async_copy(wo_columns(yy, c), wo_rows(yy, c), own_wo_sem.at[yy])
        for yy in range(NY)
    ]
    for load in own_wo:
        load.start()

    barrier = pltpu.get_barrier_semaphore()
    peers = [(s, sib), (z_peer, h)]
    peers += [(s, y_peer(d)) for d in (1, 2, 3)] + [(x_peer(d), h) for d in (1, 2, 3)]
    for seq, head in peers:
        pl.semaphore_signal(
            barrier, inc=1, device_id=(seq, head), device_id_type=pl.DeviceIdType.MESH
        )
    for kind in range(2):
        fresh_pad[kind, pl.ds(0, slots), :] = jnp.zeros((slots, HD), F32)
        fresh_pad[kind, pl.ds(2 * slots, slots), :] = jnp.zeros((slots, HD), F32)
    for side in range(2):
        va[side, :, pl.ds(HD, HD)] = jnp.ones((slots, HD), BF16)
        vfa[side, :, pl.ds(HD, HD)] = jnp.ones((rows, HD), BF16)
    acc[...] = jnp.zeros_like(acc)
    ssq[...] = jnp.zeros_like(ssq)
    l_buf[...] = jnp.zeros_like(l_buf)
    pl.semaphore_wait(barrier, len(peers))

    def ag_copy(k, source, seq, head, src=None):
        return remote(
            x_all.at[source] if src is None else src, x_all.at[source],
            ag_send.at[k], ag_recv.at[source], seq, head,
        )

    for k, d in enumerate((2, 1, 3)):
        ag_copy(k, h, s, y_peer(d), tok).start()
    ag_copy(3, h, s, sib, tok).start()
    wo_copies = [
        remote(wo_columns(yy, 1 - c), wo_rows(yy, c), wo_send.at[yy], wo_recv.at[yy], s, sib)
        for yy in range(NY)
    ]
    for copy in wo_copies:
        copy.start()

    pair_copies = [
        remote(kc, kraw.at[1], pair_send.at[0], pair_recv.at[0], x_peer(to_pair), h),
        remote(vc, va.at[1, :, pl.ds(0, HD)], pair_send.at[1], pair_recv.at[1], x_peer(to_pair), h),
    ]
    for copy in pair_copies:
        copy.start()

    length = lens[request]

    def prepare_keys(side, holder):
        for at in range(0, slots, 512):
            kT[side, pl.ds(0, HD), pl.ds(at, 512)] = kraw[side, pl.ds(at, 512), :].T
        slot = holder * slots + lax.broadcasted_iota(jnp.int32, (HD, slots), 1)
        first_row = lax.broadcasted_iota(jnp.int32, (HD, slots), 0) == 0
        hidden = jnp.logical_and(first_row, slot >= length)
        kT[side, pl.ds(HD, HD), :] = jnp.where(hidden, NEG, 0.0).astype(BF16)

    loads[4].wait()
    loads[5].wait()
    prepare_keys(0, p)
    for at in (0, 1, 2, 3, 6, 7):
        loads[at].wait()
    place = offs[request] + length + p * rows
    place = place + lax.broadcasted_iota(jnp.int32, (rows, HD), 0)
    angles = place.astype(F32) * freq_v[...]
    sign = jnp.where(lax.broadcasted_iota(jnp.int32, (rows, HD), 1) < HD // 2, -1.0, 1.0)
    cos[...] = jnp.cos(angles)
    sin[...] = jnp.sin(angles) * sign

    def project(step, unused):
        d = digit(order_code([0, 0, 1, 3, 2, 1, 3, 2]), step)
        other = digit(order_code([0, 1, 0, 0, 0, 1, 1, 1]), step)
        source = ((y + d) % NY) * 2 + (c + other) % 2

        @pl.when(step > 0)
        def _():
            ag_copy(0, source, s, sib).wait_recv()

        @pl.when(jnp.logical_and(step >= 2, step < 5))
        def _():
            ag_copy(2 + step, source, s, sib).start()

        shard = x_all[source].astype(F32)
        square = shard * shard
        ssq[...] += square[:, :HD] + square[:, HD:2 * HD] + square[:, 2 * HD:]
        scaled = (shard * gain_v[source]).astype(BF16)
        at = pl.ds(pl.multiple_of(source * width, width), width)
        acc[:, pl.ds(0, width)] += jnp.dot(scaled, wq_v[at, :], preferred_element_type=F32)
        acc[:, pl.ds(width, HD)] += jnp.dot(scaled, wk_v[at, :], preferred_element_type=F32)
        acc[:, pl.ds(width + HD, HD)] += jnp.dot(scaled, wv_v[at, :], preferred_element_type=F32)
        return unused

    lax.fori_loop(0, 8, project, 0)

    scale = lax.rsqrt(jnp.sum(ssq[...], -1, keepdims=True) * (1.0 / (width * 8)) + EPS)
    cosine = cos[...]
    sine = sin[...]

    def rope(vectors):
        return vectors * cosine + pltpu.roll(vectors, HD // 2, 1) * sine

    def kv_copy(k, block, seq):
        return remote(
            kv_all.at[:, block], kv_all.at[:, block], kv_send.at[k], kv_recv.at[block], seq, h
        )

    fresh_key = rope(acc[:, pl.ds(width, HD)] * scale).astype(BF16)
    fresh_value = (acc[:, pl.ds(width + HD, HD)] * scale).astype(BF16)
    kv_all[0, p] = fresh_key
    kv_all[1, p] = fresh_value
    kv_copy(1, p, x_peer(to_pair)).start()

    def q_copy(k, dz, j, r, to_z, seq):
        return remote(
            q_all.at[dz, 0, r], q_all.at[to_z, j, r], q_send.at[k, r], q_recv.at[to_z, j, r], seq, h
        )

    fold = LOG2E / math.sqrt(HD)
    for r in range(CHUNKS):
        window = pl.ds(r * part_rows, part_rows)
        for hd in range(heads):
            vectors = acc[window, pl.ds(hd * HD, HD)] * scale[r * part_rows:(r + 1) * part_rows]
            turned = vectors * cos[window, :] + pltpu.roll(vectors, HD // 2, 1) * sin[window, :]
            q_all[0, 0, r, pl.ds(hd * part_rows, part_rows), :] = (turned * fold).astype(BF16)
        q_copy(0, 0, 0, r, 1, z_peer).start()
        q_copy(1, 0, 1, r, 0, x_peer(to_next)).start()
    kv_copy(0, p, z_peer).start()

    kfT[0] = fresh_key.T
    vfa[0, :, pl.ds(0, HD)] = fresh_value
    for copy in pair_copies:
        copy.wait_recv()
    prepare_keys(1, px)
    kv_copy(1, px, z_peer).wait_recv()
    kfT[1] = kv_all[0, px].T
    vfa[1, :, pl.ds(0, HD)] = kv_all[1, px]

    eye = lax.broadcasted_iota(jnp.int32, (HD, HD), 0) == lax.broadcasted_iota(
        jnp.int32, (HD, HD), 1
    )
    first_lane = lax.broadcasted_iota(jnp.int32, (part_rows, HD), 1) == 0
    one_lane = jnp.where(first_lane, 1.0, 0.0).astype(BF16)
    offset = lax.broadcasted_iota(jnp.int32, (part_rows, rows), 0) - lax.broadcasted_iota(
        jnp.int32, (part_rows, rows), 1
    )

    def o_copies(dz, r):
        return (
            remote(o_buf.at[dz, 1, r], o_in.at[dz, r], o_send.at[dz, r], o_recv.at[dz, r],
                   x_peer(to_next), h),
            remote(l_buf.at[dz, 1, r], l_in.at[dz, r], l_send.at[dz, r], l_recv.at[dz, r],
                   x_peer(to_next), h),
        )

    def z_copies(r):
        return (
            remote(oz_out.at[r], oz_in.at[r], z_send.at[r], z_recv.at[r], z_peer, h),
            remote(lz_out.at[r], lz_in.at[r], lz_send.at[r], lz_recv.at[r], z_peer, h),
        )

    def weigh(logsums):
        highest = logsums[0]
        for one in logsums[1:]:
            highest = jnp.maximum(highest, one)
        shares = [jnp.exp2(one - highest) for one in logsums]
        total = shares[0]
        for one in shares[1:]:
            total = total + one
        return [one / total for one in shares], highest + jnp.log(total) * LOG2E

    def blend(parts, shares, hd):
        result = None
        for part, share in zip(parts, shares):
            column = jnp.sum(jnp.where(eye, share[hd:hd + 1, :], 0.0), 1, keepdims=True)
            term = part[pl.ds(hd * part_rows, part_rows), :].astype(F32) * column
            result = term if result is None else result + term
        return result

    def merge_for_z(r):
        for copy in o_copies(1, r):
            copy.wait_recv()
        shares, merged = weigh([l_buf[1, 0, r], l_in[1, r]])
        lz_out[r] = merged
        for hd in range(heads):
            oz_out[r, pl.ds(hd * part_rows, part_rows), :] = blend(
                [o_buf.at[1, 0, r], o_in.at[1, r]], shares, hd
            ).astype(BF16)
        for copy in z_copies(r):
            copy.start()

    def attend(step, unused):
        dz = digit(order_code([o[0] for o in ORDER]), step)
        j = digit(order_code([o[1] for o in ORDER]), step)
        r = digit(order_code([o[2] for o in ORDER]), step)
        block = 2 * ((x + j * to_next) % NX) + (zhi + dz) % 2

        for chunk in range(CHUNKS):
            @pl.when(step == STEP_FORWARD[chunk])
            def _():
                q_copy(0, 0, 0, chunk, 1, z_peer).wait_recv()
                q_copy(2, 1, 1, chunk, 1, x_peer(to_next)).start()

        @pl.when(j > 0)
        def _():
            q_copy(1, 0, 1, r, dz, z_peer).wait_recv()

        ahead = [
            offset + r * part_rows + (block - holder) * rows >= 0 for holder in (p, px)
        ]

        def score(hd, side):
            query = q_all[dz, j, r, pl.ds(hd * part_rows, part_rows), :]
            wide = jnp.concatenate([query, one_lane], 1)
            scores = [
                jnp.dot(wide, kT[side, :, pl.ds(at, CHUNK)], preferred_element_type=F32)
                for at in range(0, slots, CHUNK)
            ]
            fresh = jnp.dot(query, kfT[side], preferred_element_type=F32)
            scores.append(jnp.where(ahead[side], fresh, NEG))
            top = jnp.max(scores[0], -1, keepdims=True)
            for part in scores[1:]:
                top = jnp.maximum(top, jnp.max(part, -1, keepdims=True))
            return scores, top

        def weigh_values(side, scores, top):
            values = [va[side, pl.ds(at, CHUNK), :] for at in range(0, slots, CHUNK)]
            summed = None
            for part, value in zip(scores, values + [vfa[side]]):
                weights = jnp.exp2(part - top).astype(BF16)
                term = jnp.dot(weights, value, preferred_element_type=F32)
                summed = term if summed is None else summed + term
            return summed, top

        pieces = [(hd, side) for hd in range(heads) for side in range(2)]
        current = score(*pieces[0])
        halves = []
        for at, (hd, side) in enumerate(pieces):
            following = score(*pieces[at + 1]) if at + 1 < len(pieces) else None
            halves.append(weigh_values(side, *current))
            current = following
            if side == 1:
                (first, first_top), (second, second_top) = halves
                halves = []
                top = jnp.maximum(first_top, second_top)
                summed = first * jnp.exp2(first_top - top) + second * jnp.exp2(second_top - top)
                total = summed[:, HD:]
                o_buf[dz, j, r, pl.ds(hd * part_rows, part_rows), :] = (
                    summed[:, :HD] / total
                ).astype(BF16)
                l_buf[dz, j, r, pl.ds(hd, 1), :] = jnp.sum(
                    jnp.where(eye, top + jnp.log(total) * LOG2E, 0.0), 0, keepdims=True
                )

        @pl.when(j > 0)
        def _():
            for copy in o_copies(dz, r):
                copy.start()

        @pl.when(step == STEP_MERGE)
        def _():
            merge_for_z(0)

        return unused

    lax.fori_loop(0, len(ORDER), attend, 0)
    merge_for_z(1)

    others = (to_pair, to_next, 2)
    for k, d in ((2, to_next), (3, 2)):
        kv_copy(k, p, x_peer(d)).start()
    kv_copy(0, pz, z_peer).wait_recv()
    for k, d in enumerate(others):
        kv_copy(4 + k, pz, x_peer(d)).start()

    for load in own_wo:
        load.wait()
    for copy in wo_copies:
        copy.wait_recv()

    def att_copy(r, core):
        return remote(
            att_all.at[r, core], att_all.at[r, core], att_send.at[r], att_recv.at[r], s, sib
        )

    def pr_copy(r, d):
        back = (NY - d) % NY
        return remote(
            pr_out.at[r, d], pr_in.at[r, back], pr_send.at[r, d], pr_recv.at[r, back], s, y_peer(d)
        )

    for r in range(CHUNKS):
        for copy in o_copies(0, r):
            copy.wait_recv()
        for copy in z_copies(r):
            copy.wait_recv()
        shares, merged = weigh([l_buf[0, 0, r], l_in[0, r], lz_in[r]])
        for hd in range(heads):
            att_all[r, c, :, pl.ds(hd * HD, HD)] = blend(
                [o_buf.at[0, 0, r], o_in.at[0, r], oz_in.at[r]], shares, hd
            ).astype(BF16)
        att_copy(r, c).start()
        att_copy(r, 1 - c).wait_recv()
        both = jnp.concatenate([att_all[r, 0], att_all[r, 1]], 1)
        for d in (2, 1, 3):
            part = jnp.dot(both, wo_all[(y + d) % NY], preferred_element_type=F32)
            pr_out[r, d] = part.astype(BF16)
            pr_copy(r, d).start()
        own_part[r] = jnp.dot(both, wo_all[y], preferred_element_type=F32)

    for d in (to_next, 2):
        kv_copy(0, 2 * ((x + d) % NX) + zhi, z_peer).wait_recv()
    for d in others:
        kv_copy(0, 2 * ((x + d) % NX) + (zhi + 1) % 2, z_peer).wait_recv()
    for kind in range(2):
        for block in range(GROUP):
            fresh_pad[kind, pl.ds(slots + block * rows, rows), :] = kv_all[kind, block].astype(F32)
    start = p * slots - length
    begin = jnp.clip(start + slots, 0, 2 * slots)

    def place_rows(i, unused):
        at = pl.ds(pl.multiple_of(i * rows, rows), rows)
        token = start + i * rows + lax.broadcasted_iota(jnp.int32, (rows, HD), 0)
        written = jnp.logical_and(token >= 0, token < GROUP * rows)
        window = pl.ds(begin + i * rows, rows)
        for kind in range(2):
            cached = kraw[0, at, :] if kind == 0 else va[0, at, pl.ds(0, HD)]
            fresh = fresh_pad[kind, window, :].astype(BF16)
            updated[kind, at, :] = jnp.where(written, fresh, cached)
        return unused

    lax.fori_loop(0, GROUP, place_rows, 0)
    stores = [
        pltpu.make_async_copy(updated.at[0], keys_out, out_sem.at[0]),
        pltpu.make_async_copy(updated.at[1], values_out, out_sem.at[1]),
    ]
    for store in stores:
        store.start()

    for r in range(CHUNKS):
        result = own_part[r]
        for d in (1, 3, 2):
            pr_copy(r, (NY - d) % NY).wait_recv()
        for d in (1, 2, 3):
            result = result + pr_in[r, d].astype(F32)
        out[pl.ds(r * part_rows, part_rows), :] = result.astype(BF16)

    for k in range(3):
        ag_copy(k, h, s, sib, tok).wait_send()
    ag_copy(3, h, s, sib, tok).wait_send()
    for k in range(4, 7):
        ag_copy(k, h, s, sib).wait_send()
    for copy in wo_copies:
        copy.wait_send()
    for copy in pair_copies:
        copy.wait_send()
    for k in range(7):
        kv_copy(k, p, z_peer).wait_send()
    for r in range(CHUNKS):
        for k in range(3):
            q_copy(k, 0, 0, r, 1, z_peer).wait_send()
        for copy in o_copies(0, r) + o_copies(1, r) + z_copies(r):
            copy.wait_send()
        att_copy(r, c).wait_send()
        for d in (1, 2, 3):
            pr_copy(r, d).wait_send()
    for store in stores:
        store.wait()


def hand_on(*refs):
    sems = refs[6]
    copies = [pltpu.make_async_copy(refs[0], refs[3], sems.at[8])]
    for at in (1, 2):
        share = refs[at].shape[0] // 4
        for quarter in range(4):
            window = pl.ds(quarter * share, share)
            copies.append(
                pltpu.make_async_copy(
                    refs[at].at[window], refs[at + 3].at[window], sems.at[4 * at - 4 + quarter]
                )
            )
    for copy in copies:
        copy.start()
    for copy in copies:
        copy.wait()


def shards(
    tokens, norm_gain, w_query, w_key, w_value, w_out, keys_cache, values_cache,
    cached_lengths, rope_offsets,
):
    rows, width = tokens.shape
    slots = keys_cache.shape[0]
    heads = width // HD
    half = np.arange(HD) % (HD // 2)
    frequency = (ROPE_BASE ** (-half * 2.0 / HD)).astype(np.float32)[None]

    hbm_spec = pl.BlockSpec(memory_space=pltpu.HBM)
    vmem_spec = pl.BlockSpec(memory_space=pltpu.VMEM)
    smem_spec = pl.BlockSpec(memory_space=pltpu.SMEM)
    dma = pltpu.SemaphoreType.DMA
    block = (heads * rows // CHUNKS, HD)
    results = pl.pallas_call(
        kernel,
        out_shape=(
            jax.ShapeDtypeStruct((rows, width), BF16),
            jax.ShapeDtypeStruct((slots, HD), BF16),
            jax.ShapeDtypeStruct((slots, HD), BF16),
        ),
        in_specs=[hbm_spec] * 9 + [smem_spec] * 2,
        out_specs=(vmem_spec, hbm_spec, hbm_spec),
        scratch_shapes=[
            pltpu.VMEM((8, rows, width), BF16),
            pltpu.VMEM((8, 1, width), F32),
            pltpu.VMEM((1, HD), F32),
            pltpu.VMEM(w_query.shape, BF16),
            pltpu.VMEM(w_key.shape, BF16),
            pltpu.VMEM(w_value.shape, BF16),
            pltpu.VMEM((NY, 2 * width, width), BF16),
            pltpu.VMEM((2, slots, HD), BF16),
            pltpu.VMEM((2, 2 * HD, slots), BF16),
            pltpu.VMEM((2, slots, 2 * HD), BF16),
            pltpu.VMEM((2, HD, rows), BF16),
            pltpu.VMEM((2, rows, 2 * HD), BF16),
            pltpu.VMEM((rows, width + 2 * HD), F32),
            pltpu.VMEM((rows, HD), F32),
            pltpu.VMEM((rows, HD), F32),
            pltpu.VMEM((rows, HD), F32),
            pltpu.VMEM((2, 3 * slots, HD), F32),
            pltpu.VMEM((2, slots, HD), BF16),
            pltpu.VMEM((2, 2, CHUNKS) + block, BF16),
            pltpu.VMEM((2, GROUP, rows, HD), BF16),
            pltpu.VMEM((2, 2, CHUNKS) + block, BF16),
            pltpu.VMEM((2, 2, CHUNKS, 8, HD), F32),
            pltpu.VMEM((2, CHUNKS) + block, BF16),
            pltpu.VMEM((2, CHUNKS, 8, HD), F32),
            pltpu.VMEM((CHUNKS,) + block, BF16),
            pltpu.VMEM((CHUNKS, 8, HD), F32),
            pltpu.VMEM((CHUNKS,) + block, BF16),
            pltpu.VMEM((CHUNKS, 8, HD), F32),
            pltpu.VMEM((CHUNKS, 2, rows // CHUNKS, width), BF16),
            pltpu.VMEM((CHUNKS, NY, rows // CHUNKS, width), BF16),
            pltpu.VMEM((CHUNKS, NY, rows // CHUNKS, width), BF16),
            pltpu.VMEM((CHUNKS, rows // CHUNKS, width), F32),
            dma((8,)), dma((NY,)), dma((7,)), dma((8,)), dma((NY,)), dma((NY,)), dma((2,)), dma((2,)),
            dma((3, CHUNKS)), dma((2, 2, CHUNKS)), dma((7,)), dma((GROUP,)),
            dma((2, CHUNKS)), dma((2, CHUNKS)), dma((2, CHUNKS)), dma((2, CHUNKS)),
            dma((CHUNKS,)), dma((CHUNKS,)), dma((CHUNKS,)), dma((CHUNKS,)),
            dma((CHUNKS,)), dma((CHUNKS,)), dma((CHUNKS, NY)), dma((CHUNKS, NY)), dma((2,)),
        ],
        compiler_params=pltpu.CompilerParams(
            collective_id=0, has_side_effects=True, vmem_limit_bytes=64 << 20
        ),
        name="span_attention",
    )(
        tokens, norm_gain.reshape(8, 1, width), w_query, w_key, w_value, w_out,
        keys_cache, values_cache, frequency, cached_lengths, rope_offsets,
    )
    return pl.pallas_call(
        hand_on,
        out_shape=tuple(jax.ShapeDtypeStruct(one.shape, one.dtype) for one in results),
        in_specs=[hbm_spec] * 3,
        out_specs=(hbm_spec,) * 3,
        scratch_shapes=[dma((9,))],
        name="hand_on",
    )(*results)


def solution(mesh):
    return jax.shard_map(
        shards,
        mesh=mesh,
        in_specs=(
            P("seq", "head"), P(), P(None, "head"), P(None, "head"), P(None, "head"),
            P("head", None), P("seq", "head"), P("seq", "head"), P(), P(),
        ),
        out_specs=(P("seq", "head"), P("seq", "head"), P("seq", "head")),
        check_vma=False,
    )
```

time: 115 us -> 113 us (0.983)
  the two profiles are of different devices: /device:TPU:35 before, /device:TPU:1 now
where the time goes in v2:
time: 113 us
  Pallas kernels  112 us (99%)
    pallas_call x1, Pallas kernels, shards(): pl.pallas_call(kernel, out_shape=(jax.ShapeDtypeStruct((rows, width), BF1...  73.3 us
    pallas_call x1, Pallas kernels, shards(): pl.pallas_call(hand_on, out_shape=tuple((jax.ShapeDtypeStruct(one.shape,...  38.9 us

profile of v2, /device:TPU:1, one launch (start us, length us, event | category | flops | bytes accessed | tf_op | source)
XLA Modules:
  0.0 112.9 jit_solution(11150810879797100847)
XLA Ops:
  0.6 73.3 %span_attention.1 = (bf16[256,384]{1,0:T(8,128)(2,1)}, bf16[2048,128]{1,0:T(8,128)(2,1)}, bf16[2048,128]{1,0:T(8,128)(2,1)}) custom-call(bf16[256,384]{1,0:T(8,128)(2,1)} %tok.1, f32[8,1,384]{2,1,0:T(1,128)} %bitcast.1, bf16[3072,384]{1,0:T(8,128)(2,1)} %wq.1, bf16[3072,128]{1,0:T(8,128)(2,1)} %wk.1, bf16[3072,128]{1,0:T(8,128)(2,1)} %wv.1, ...), custom_call_target="tpu_custom_call" | custom-call | tf_op jit(solution)/shard_map/span_attention/pallas_call | solution.py:507
  74.0 38.9 %hand_on.1 = (bf16[256,384]{1,0:T(8,128)(2,1)}, bf16[2048,128]{1,0:T(8,128)(2,1)}, bf16[2048,128]{1,0:T(8,128)(2,1)}) custom-call(bf16[256,384]{1,0:T(8,128)(2,1)} %get-tuple-element.6.refs_0_, bf16[2048,128]{1,0:T(8,128)(2,1)} %get-tuple-element.7.refs_1_, bf16[2048,128]{1,0:T(8,128)(2,1)} %get-tuple-element.8.refs_2_), custom_call_target="tpu_custom_call" | custom-call | tf_op jit(solution)/shard_map/hand_on/pallas_call | solution.py:563

commit v3 on v2

--- a/solution.py
+++ b/solution.py
@@ -24,9 +24,9 @@
 def digit(number, place):
     value = number
     result = value % 10
-    for at in range(1, 8):
+    for at in range(1, 16):
         value = value // 10
-        flag = (place + 8 - at) // 8 - (place + 7 - at) // 8
+        flag = (place + 16 - at) // 16 - (place + 15 - at) // 16
         result = result + flag * (value % 10 - number % 10)
     return result
 
@@ -35,11 +35,14 @@
     return sum(d * 10**i for i, d in enumerate(digits))
 
 
-ORDER = [(0, 0, 0), (0, 0, 1), (0, 1, 0), (1, 0, 0), (1, 1, 0), (1, 0, 1), (1, 1, 1), (0, 1, 1)]
-STEP_FORWARD = (3, 5)
-STEP_MERGE = 5
+ORDER = [(0, 0, 0), (0, 0, 1), (0, 0, 2), (0, 0, 3)]
+ORDER += [(1, j, r) for r in range(4) for j in range(2)]
+ORDER += [(0, 1, 0), (0, 1, 1), (0, 1, 2), (0, 1, 3)]
+STEP_FORWARD = (3, 4, 6, 8)
+STEP_MERGE = (7, 9, 11, 13)
 CHUNK = 1024
-CHUNKS = 2
+CHUNKS = 4
+GROUPS = 2
 
 
 def kernel(
@@ -92,8 +95,7 @@
         pltpu.make_async_copy(gain, gain_v, load_sem.at[6]),
         pltpu.make_async_copy(freq, freq_v, load_sem.at[7]),
     ]
-    for load in loads:
-        load.start()
+    loads[0].start()
 
     def wo_columns(yy, cc):
         return wo.at[:, pl.ds(pl.multiple_of((yy * 2 + cc) * width, width), width)]
@@ -105,9 +107,6 @@
         pltpu.make_async_copy(wo_columns(yy, c), wo_rows(yy, c), own_wo_sem.at[yy])
         for yy in range(NY)
     ]
-    for load in own_wo:
-        load.start()
-
     barrier = pltpu.get_barrier_semaphore()
     peers = [(s, sib), (z_peer, h)]
     peers += [(s, y_peer(d)) for d in (1, 2, 3)] + [(x_peer(d), h) for d in (1, 2, 3)]
@@ -139,15 +138,14 @@
         remote(wo_columns(yy, 1 - c), wo_rows(yy, c), wo_send.at[yy], wo_recv.at[yy], s, sib)
         for yy in range(NY)
     ]
-    for copy in wo_copies:
-        copy.start()
-
     pair_copies = [
         remote(kc, kraw.at[1], pair_send.at[0], pair_recv.at[0], x_peer(to_pair), h),
         remote(vc, va.at[1, :, pl.ds(0, HD)], pair_send.at[1], pair_recv.at[1], x_peer(to_pair), h),
     ]
     for copy in pair_copies:
         copy.start()
+    for load in loads[1:] + own_wo:
+        load.start()
 
     length = lens[request]
 
@@ -229,6 +227,8 @@
         q_copy(0, 0, 0, r, 1, z_peer).start()
         q_copy(1, 0, 1, r, 0, x_peer(to_next)).start()
     kv_copy(0, p, z_peer).start()
+    for copy in wo_copies:
+        copy.start()
 
     kfT[0] = fresh_key.T
     vfa[0, :, pl.ds(0, HD)] = fresh_value
@@ -239,14 +239,14 @@
     kfT[1] = kv_all[0, px].T
     vfa[1, :, pl.ds(0, HD)] = kv_all[1, px]
 
-    eye = lax.broadcasted_iota(jnp.int32, (HD, HD), 0) == lax.broadcasted_iota(
-        jnp.int32, (HD, HD), 1
+    eye = lax.broadcasted_iota(jnp.int32, (part_rows, HD), 0) == lax.broadcasted_iota(
+        jnp.int32, (part_rows, HD), 1
     )
-    first_lane = lax.broadcasted_iota(jnp.int32, (part_rows, HD), 1) == 0
+    stacked = heads * part_rows
+    first_lane = lax.broadcasted_iota(jnp.int32, (stacked, HD), 1) == 0
     one_lane = jnp.where(first_lane, 1.0, 0.0).astype(BF16)
-    offset = lax.broadcasted_iota(jnp.int32, (part_rows, rows), 0) - lax.broadcasted_iota(
-        jnp.int32, (part_rows, rows), 1
-    )
+    offset = lax.broadcasted_iota(jnp.int32, (stacked, rows), 0) % part_rows
+    offset = offset - lax.broadcasted_iota(jnp.int32, (stacked, rows), 1)
 
     def o_copies(dz, r):
         return (
@@ -312,62 +312,61 @@
             offset + r * part_rows + (block - holder) * rows >= 0 for holder in (p, px)
         ]
 
-        def score(hd, side):
-            query = q_all[dz, j, r, pl.ds(hd * part_rows, part_rows), :]
-            wide = jnp.concatenate([query, one_lane], 1)
-            scores = [
-                jnp.dot(wide, kT[side, :, pl.ds(at, CHUNK)], preferred_element_type=F32)
-                for at in range(0, slots, CHUNK)
-            ]
-            fresh = jnp.dot(query, kfT[side], preferred_element_type=F32)
-            scores.append(jnp.where(ahead[side], fresh, NEG))
+        query = q_all[dz, j, r]
+        wide = jnp.concatenate([query, one_lane], 1)
+
+        def score(side, at):
+            scores = [jnp.dot(wide, kT[side, :, pl.ds(at, CHUNK)], preferred_element_type=F32)]
+            if at + CHUNK == slots:
+                fresh = jnp.dot(query, kfT[side], preferred_element_type=F32)
+                scores.append(jnp.where(ahead[side], fresh, NEG))
             top = jnp.max(scores[0], -1, keepdims=True)
             for part in scores[1:]:
                 top = jnp.maximum(top, jnp.max(part, -1, keepdims=True))
             return scores, top
 
-        def weigh_values(side, scores, top):
-            values = [va[side, pl.ds(at, CHUNK), :] for at in range(0, slots, CHUNK)]
+        def weigh_values(side, at, scores, top):
             summed = None
-            for part, value in zip(scores, values + [vfa[side]]):
+            for part, value in zip(scores, (va[side, pl.ds(at, CHUNK), :], vfa[side])):
                 weights = jnp.exp2(part - top).astype(BF16)
                 term = jnp.dot(weights, value, preferred_element_type=F32)
                 summed = term if summed is None else summed + term
             return summed, top
 
-        pieces = [(hd, side) for hd in range(heads) for side in range(2)]
+        pieces = [(side, at) for side in range(2) for at in range(0, slots, CHUNK)]
         current = score(*pieces[0])
-        halves = []
-        for at, (hd, side) in enumerate(pieces):
-            following = score(*pieces[at + 1]) if at + 1 < len(pieces) else None
-            halves.append(weigh_values(side, *current))
+        sums = []
+        for number, piece in enumerate(pieces):
+            following = score(*pieces[number + 1]) if number + 1 < len(pieces) else None
+            sums.append(weigh_values(*piece, *current))
             current = following
-            if side == 1:
-                (first, first_top), (second, second_top) = halves
-                halves = []
-                top = jnp.maximum(first_top, second_top)
-                summed = first * jnp.exp2(first_top - top) + second * jnp.exp2(second_top - top)
-                total = summed[:, HD:]
-                o_buf[dz, j, r, pl.ds(hd * part_rows, part_rows), :] = (
-                    summed[:, :HD] / total
-                ).astype(BF16)
-                l_buf[dz, j, r, pl.ds(hd, 1), :] = jnp.sum(
-                    jnp.where(eye, top + jnp.log(total) * LOG2E, 0.0), 0, keepdims=True
-                )
+        top = sums[0][1]
+        for one, one_top in sums[1:]:
+            top = jnp.maximum(top, one_top)
+        summed = sums[0][0] * jnp.exp2(sums[0][1] - top)
+        for one, one_top in sums[1:]:
+            summed = summed + one * jnp.exp2(one_top - top)
+        total = summed[:, HD:]
+        o_buf[dz, j, r] = (summed[:, :HD] / total).astype(BF16)
+        logsum = top + jnp.log(total) * LOG2E
+        for hd in range(heads):
+            l_buf[dz, j, r, pl.ds(hd, 1), :] = jnp.sum(
+                jnp.where(eye, logsum[hd * part_rows:(hd + 1) * part_rows], 0.0), 0, keepdims=True
+            )
 
         @pl.when(j > 0)
         def _():
             for copy in o_copies(dz, r):
                 copy.start()
 
-        @pl.when(step == STEP_MERGE)
-        def _():
-            merge_for_z(0)
+        for chunk in range(CHUNKS):
+            @pl.when(step == STEP_MERGE[chunk])
+            def _():
+                merge_for_z(chunk)
 
         return unused
 
     lax.fori_loop(0, len(ORDER), attend, 0)
-    merge_for_z(1)
 
     others = (to_pair, to_next, 2)
     for k, d in ((2, to_next), (3, 2)):
@@ -392,24 +391,27 @@
             pr_out.at[r, d], pr_in.at[r, back], pr_send.at[r, d], pr_recv.at[r, back], s, y_peer(d)
         )
 
-    for r in range(CHUNKS):
-        for copy in o_copies(0, r):
-            copy.wait_recv()
-        for copy in z_copies(r):
-            copy.wait_recv()
-        shares, merged = weigh([l_buf[0, 0, r], l_in[0, r], lz_in[r]])
-        for hd in range(heads):
-            att_all[r, c, :, pl.ds(hd * HD, HD)] = blend(
-                [o_buf.at[0, 0, r], o_in.at[0, r], oz_in.at[r]], shares, hd
-            ).astype(BF16)
-        att_copy(r, c).start()
-        att_copy(r, 1 - c).wait_recv()
-        both = jnp.concatenate([att_all[r, 0], att_all[r, 1]], 1)
+    per_group = CHUNKS // GROUPS
+    for g in range(GROUPS):
+        for k in range(per_group):
+            r = g * per_group + k
+            for copy in o_copies(0, r):
+                copy.wait_recv()
+            for copy in z_copies(r):
+                copy.wait_recv()
+            shares, merged = weigh([l_buf[0, 0, r], l_in[0, r], lz_in[r]])
+            for hd in range(heads):
+                att_all[g, c, pl.ds(k * part_rows, part_rows), pl.ds(hd * HD, HD)] = blend(
+                    [o_buf.at[0, 0, r], o_in.at[0, r], oz_in.at[r]], shares, hd
+                ).astype(BF16)
+        att_copy(g, c).start()
+        att_copy(g, 1 - c).wait_recv()
+        both = jnp.concatenate([att_all[g, 0], att_all[g, 1]], 1)
         for d in (2, 1, 3):
             part = jnp.dot(both, wo_all[(y + d) % NY], preferred_element_type=F32)
-            pr_out[r, d] = part.astype(BF16)
-            pr_copy(r, d).start()
-        own_part[r] = jnp.dot(both, wo_all[y], preferred_element_type=F32)
+            pr_out[g, d] = part.astype(BF16)
+            pr_copy(g, d).start()
+        own_part[g] = jnp.dot(both, wo_all[y], preferred_element_type=F32)
 
     for d in (to_next, 2):
         kv_copy(0, 2 * ((x + d) % NX) + zhi, z_peer).wait_recv()
@@ -440,13 +442,13 @@
     for store in stores:
         store.start()
 
-    for r in range(CHUNKS):
-        result = own_part[r]
+    for g in range(GROUPS):
+        result = own_part[g]
         for d in (1, 3, 2):
-            pr_copy(r, (NY - d) % NY).wait_recv()
+            pr_copy(g, (NY - d) % NY).wait_recv()
         for d in (1, 2, 3):
-            result = result + pr_in[r, d].astype(F32)
-        out[pl.ds(r * part_rows, part_rows), :] = result.astype(BF16)
+            result = result + pr_in[g, d].astype(F32)
+        out[pl.ds(g * (rows // GROUPS), rows // GROUPS), :] = result.astype(BF16)
 
     for k in range(3):
         ag_copy(k, h, s, sib, tok).wait_send()
@@ -464,28 +466,34 @@
             q_copy(k, 0, 0, r, 1, z_peer).wait_send()
         for copy in o_copies(0, r) + o_copies(1, r) + z_copies(r):
             copy.wait_send()
-        att_copy(r, c).wait_send()
+    for g in range(GROUPS):
+        att_copy(g, c).wait_send()
         for d in (1, 2, 3):
-            pr_copy(r, d).wait_send()
+            pr_copy(g, d).wait_send()
     for store in stores:
         store.wait()
 
 
 def hand_on(*refs):
-    sems = refs[6]
-    copies = [pltpu.make_async_copy(refs[0], refs[3], sems.at[8])]
-    for at in (1, 2):
-        share = refs[at].shape[0] // 4
-        for quarter in range(4):
-            window = pl.ds(quarter * share, share)
-            copies.append(
-                pltpu.make_async_copy(
-                    refs[at].at[window], refs[at + 3].at[window], sems.at[4 * at - 4 + quarter]
-                )
-            )
-    for copy in copies:
+    sources, targets, held, (in_sem, out_sem) = refs[:3], refs[3:6], refs[6:9], refs[9:]
+    pieces = []
+    for at, source in enumerate(sources):
+        share = source.shape[0] // 2
+        pieces += [(at, half, pl.ds(half * share, share)) for half in range(2)]
+    arriving = [
+        pltpu.make_async_copy(sources[at].at[window], held[at].at[window], in_sem.at[at, half])
+        for at, half, window in pieces
+    ]
+    leaving = [
+        pltpu.make_async_copy(held[at].at[window], targets[at].at[window], out_sem.at[at, half])
+        for at, half, window in pieces
+    ]
+    for copy in arriving:
         copy.start()
-    for copy in copies:
+    for first, second in zip(arriving, leaving):
+        first.wait()
+        second.start()
+    for copy in leaving:
         copy.wait()
 
 
@@ -542,15 +550,15 @@
             pltpu.VMEM((CHUNKS, 8, HD), F32),
             pltpu.VMEM((CHUNKS,) + block, BF16),
             pltpu.VMEM((CHUNKS, 8, HD), F32),
-            pltpu.VMEM((CHUNKS, 2, rows // CHUNKS, width), BF16),
-            pltpu.VMEM((CHUNKS, NY, rows // CHUNKS, width), BF16),
-            pltpu.VMEM((CHUNKS, NY, rows // CHUNKS, width), BF16),
-            pltpu.VMEM((CHUNKS, rows // CHUNKS, width), F32),
+            pltpu.VMEM((GROUPS, 2, rows // GROUPS, width), BF16),
+            pltpu.VMEM((GROUPS, NY, rows // GROUPS, width), BF16),
+            pltpu.VMEM((GROUPS, NY, rows // GROUPS, width), BF16),
+            pltpu.VMEM((GROUPS, rows // GROUPS, width), F32),
             dma((8,)), dma((NY,)), dma((7,)), dma((8,)), dma((NY,)), dma((NY,)), dma((2,)), dma((2,)),
             dma((3, CHUNKS)), dma((2, 2, CHUNKS)), dma((7,)), dma((GROUP,)),
             dma((2, CHUNKS)), dma((2, CHUNKS)), dma((2, CHUNKS)), dma((2, CHUNKS)),
             dma((CHUNKS,)), dma((CHUNKS,)), dma((CHUNKS,)), dma((CHUNKS,)),
-            dma((CHUNKS,)), dma((CHUNKS,)), dma((CHUNKS, NY)), dma((CHUNKS, NY)), dma((2,)),
+            dma((GROUPS,)), dma((GROUPS,)), dma((GROUPS, NY)), dma((GROUPS, NY)), dma((2,)),
         ],
         compiler_params=pltpu.CompilerParams(
             collective_id=0, has_side_effects=True, vmem_limit_bytes=64 << 20
@@ -565,7 +573,8 @@
         out_shape=tuple(jax.ShapeDtypeStruct(one.shape, one.dtype) for one in results),
         in_specs=[hbm_spec] * 3,
         out_specs=(hbm_spec,) * 3,
-        scratch_shapes=[dma((9,))],
+        scratch_shapes=[pltpu.VMEM(one.shape, one.dtype) for one in results]
+        + [dma((3, 2)), dma((3, 2))],
         name="hand_on",
     )(*results)
 

time: 113 us -> 74.7 us (0.66)
  Pallas kernels: 112 us -> 74 us
    pallas_call x1, Pallas kernels: 38.9 us -> 2.12 us  [shards(): pl.pallas_call(hand_on, out_shape=tuple((jax.ShapeDtypeStruct(one.shape,...]
    pallas_call x1, Pallas kernels: 73.3 us -> 71.8 us  [shards(): pl.pallas_call(kernel, out_shape=(jax.ShapeDtypeStruct((rows, width), BF1...]
where the time goes in v3:
time: 74.7 us; the launch traced here: 74.6 us
  Pallas kernels  74 us (99%)
    pallas_call x1, Pallas kernels, shards(): pl.pallas_call(kernel, out_shape=(jax.ShapeDtypeStruct((rows, width), BF1...  71.8 us
    pallas_call x1, Pallas kernels, shards(): pl.pallas_call(hand_on, out_shape=tuple((jax.ShapeDtypeStruct(one.shape,...  2.12 us

profile of v3, /device:TPU:1, one launch (start us, length us, event | category | flops | bytes accessed | tf_op | source)
XLA Modules:
  0.0 74.6 jit_solution(14325638968139979836)
XLA Ops:
  0.6 71.8 %span_attention.1 = (bf16[256,384]{1,0:T(8,128)(2,1)}, bf16[2048,128]{1,0:T(8,128)(2,1)}, bf16[2048,128]{1,0:T(8,128)(2,1)}) custom-call(bf16[256,384]{1,0:T(8,128)(2,1)} %tok.1, f32[8,1,384]{2,1,0:T(1,128)} %bitcast.1, bf16[3072,384]{1,0:T(8,128)(2,1)} %wq.1, bf16[3072,128]{1,0:T(8,128)(2,1)} %wk.1, bf16[3072,128]{1,0:T(8,128)(2,1)} %wv.1, ...), custom_call_target="tpu_custom_call" | custom-call | tf_op jit(solution)/shard_map/span_attention/pallas_call | solution.py:515
  72.5 2.1 %hand_on.1 = (bf16[256,384]{1,0:T(8,128)(2,1)}, bf16[2048,128]{1,0:T(8,128)(2,1)}, bf16[2048,128]{1,0:T(8,128)(2,1)}) custom-call(bf16[256,384]{1,0:T(8,128)(2,1)} %get-tuple-element.6.refs_0_, bf16[2048,128]{1,0:T(8,128)(2,1)} %get-tuple-element.7.refs_1_, bf16[2048,128]{1,0:T(8,128)(2,1)} %get-tuple-element.8.refs_2_), custom_call_target="tpu_custom_call" | custom-call | tf_op jit(solution)/shard_map/hand_on/pallas_call | solution.py:571

commit v4 on v3

--- a/solution.py
+++ b/solution.py
@@ -35,12 +35,14 @@
     return sum(d * 10**i for i, d in enumerate(digits))
 
 
-ORDER = [(0, 0, 0), (0, 0, 1), (0, 0, 2), (0, 0, 3)]
-ORDER += [(1, j, r) for r in range(4) for j in range(2)]
-ORDER += [(0, 1, 0), (0, 1, 1), (0, 1, 2), (0, 1, 3)]
-STEP_FORWARD = (3, 4, 6, 8)
-STEP_MERGE = (7, 9, 11, 13)
-CHUNK = 1024
+ORDER = [(0, 0, 0), (0, 0, 1), (0, 1, 0), (0, 1, 1), (1, 0, 0), (1, 1, 0), (1, 1, 1), (1, 0, 1)]
+ORDER += [(1, 1, 2), (1, 0, 2), (1, 1, 3), (1, 0, 3), (0, 1, 2), (0, 1, 3), (0, 0, 2), (0, 0, 3)]
+LATE_FRESH = 2
+STEP_FORWARD = (4, 5, 6, 8)
+STEP_MERGE = (6, 8, 10, 11)
+STEP_KEYS = 6
+STEP_BLEND, STEP_PROJECT = 13, 14
+CHUNK = 2048
 CHUNKS = 4
 GROUPS = 2
 
@@ -50,7 +52,7 @@
     out, keys_out, values_out,
     x_all, gain_v, freq_v, wq_v, wk_v, wv_v, wo_all, kraw, kT, va, kfT, vfa, acc, ssq,
     cos, sin, fresh_pad, updated, q_all, kv_all, o_buf, l_buf, o_in, l_in,
-    oz_out, lz_out, oz_in, lz_in, att_all, pr_out, pr_in, own_part,
+    oz_out, lz_out, oz_in, lz_in, att_all, pr_out, pr_in, own_part, late_o, late_l,
     load_sem, own_wo_sem, ag_send, ag_recv, wo_send, wo_recv, pair_send, pair_recv,
     q_send, q_recv, kv_send, kv_recv, o_send, o_recv, l_send, l_recv,
     z_send, z_recv, lz_send, lz_recv, att_send, att_recv, pr_send, pr_recv, out_sem,
@@ -123,6 +125,7 @@
     acc[...] = jnp.zeros_like(acc)
     ssq[...] = jnp.zeros_like(ssq)
     l_buf[...] = jnp.zeros_like(l_buf)
+    late_l[...] = jnp.zeros_like(late_l)
     pl.semaphore_wait(barrier, len(peers))
 
     def ag_copy(k, source, seq, head, src=None):
@@ -201,16 +204,18 @@
     def rope(vectors):
         return vectors * cosine + pltpu.roll(vectors, HD // 2, 1) * sine
 
-    def kv_copy(k, block, seq):
+    def kv_copy(kind, k, block, seq):
         return remote(
-            kv_all.at[:, block], kv_all.at[:, block], kv_send.at[k], kv_recv.at[block], seq, h
+            kv_all.at[kind, block], kv_all.at[kind, block],
+            kv_send.at[kind, k], kv_recv.at[kind, block], seq, h,
         )
 
     fresh_key = rope(acc[:, pl.ds(width, HD)] * scale).astype(BF16)
     fresh_value = (acc[:, pl.ds(width + HD, HD)] * scale).astype(BF16)
     kv_all[0, p] = fresh_key
     kv_all[1, p] = fresh_value
-    kv_copy(1, p, x_peer(to_pair)).start()
+    for kind in range(2):
+        kv_copy(kind, 1, p, x_peer(to_pair)).start()
 
     def q_copy(k, dz, j, r, to_z, seq):
         return remote(
@@ -226,7 +231,6 @@
             q_all[0, 0, r, pl.ds(hd * part_rows, part_rows), :] = (turned * fold).astype(BF16)
         q_copy(0, 0, 0, r, 1, z_peer).start()
         q_copy(1, 0, 1, r, 0, x_peer(to_next)).start()
-    kv_copy(0, p, z_peer).start()
     for copy in wo_copies:
         copy.start()
 
@@ -235,9 +239,8 @@
     for copy in pair_copies:
         copy.wait_recv()
     prepare_keys(1, px)
-    kv_copy(1, px, z_peer).wait_recv()
-    kfT[1] = kv_all[0, px].T
-    vfa[1, :, pl.ds(0, HD)] = kv_all[1, px]
+    kfT[1] = jnp.zeros((HD, rows), BF16)
+    vfa[1, :, pl.ds(0, HD)] = jnp.zeros((rows, HD), BF16)
 
     eye = lax.broadcasted_iota(jnp.int32, (part_rows, HD), 0) == lax.broadcasted_iota(
         jnp.int32, (part_rows, HD), 1
@@ -292,6 +295,66 @@
         for copy in z_copies(r):
             copy.start()
 
+    def att_copy(g, core):
+        return remote(
+            att_all.at[g, core], att_all.at[g, core], att_send.at[g], att_recv.at[g], s, sib
+        )
+
+    def pr_copy(g, d):
+        back = (NY - d) % NY
+        return remote(
+            pr_out.at[g, d], pr_in.at[g, back], pr_send.at[g, d], pr_recv.at[g, back], s, y_peer(d)
+        )
+
+    def attend_late_fresh():
+        for r in range(LATE_FRESH):
+            scores = jnp.dot(q_all[0, 0, r], kfT[1], preferred_element_type=F32)
+            scores = jnp.where(offset + r * part_rows + (p - px) * rows >= 0, scores, NEG)
+            top = jnp.max(scores, -1, keepdims=True)
+            weights = jnp.exp2(scores - top).astype(BF16)
+            summed = jnp.dot(weights, vfa[1], preferred_element_type=F32)
+            total = summed[:, HD:]
+            late_o[r] = (summed[:, :HD] / total).astype(BF16)
+            logsum = top + jnp.log(total) * LOG2E
+            for hd in range(heads):
+                late_l[r, pl.ds(hd, 1), :] = jnp.sum(
+                    jnp.where(eye, logsum[hd * part_rows:(hd + 1) * part_rows], 0.0),
+                    0, keepdims=True,
+                )
+
+    per_group = CHUNKS // GROUPS
+
+    def blend_group(g):
+        for k in range(per_group):
+            r = g * per_group + k
+            for copy in o_copies(0, r) + z_copies(r):
+                copy.wait_recv()
+            parts = [o_buf.at[0, 0, r], o_in.at[0, r], oz_in.at[r]]
+            logsums = [l_buf[0, 0, r], l_in[0, r], lz_in[r]]
+            if r < LATE_FRESH:
+                parts.append(late_o.at[r])
+                logsums.append(late_l[r])
+            shares, merged = weigh(logsums)
+            for hd in range(heads):
+                att_all[g, c, pl.ds(k * part_rows, part_rows), pl.ds(hd * HD, HD)] = blend(
+                    parts, shares, hd
+                ).astype(BF16)
+        att_copy(g, c).start()
+
+    def project_group(g):
+        if g == 0:
+            for load in own_wo:
+                load.wait()
+            for copy in wo_copies:
+                copy.wait_recv()
+        att_copy(g, 1 - c).wait_recv()
+        both = jnp.concatenate([att_all[g, 0], att_all[g, 1]], 1)
+        for d in (2, 1, 3):
+            part = jnp.dot(both, wo_all[(y + d) % NY], preferred_element_type=F32)
+            pr_out[g, d] = part.astype(BF16)
+            pr_copy(g, d).start()
+        own_part[g] = jnp.dot(both, wo_all[y], preferred_element_type=F32)
+
     def attend(step, unused):
         dz = digit(order_code([o[0] for o in ORDER]), step)
         j = digit(order_code([o[1] for o in ORDER]), step)
@@ -304,12 +367,25 @@
                 q_copy(0, 0, 0, chunk, 1, z_peer).wait_recv()
                 q_copy(2, 1, 1, chunk, 1, x_peer(to_next)).start()
 
+        @pl.when(step == STEP_KEYS)
+        def _():
+            kv_copy(0, 0, p, z_peer).start()
+
+        @pl.when(step == LATE_FRESH)
+        def _():
+            for kind in range(2):
+                kv_copy(kind, 1, px, z_peer).wait_recv()
+            kfT[1] = kv_all[0, px].T
+            vfa[1, :, pl.ds(0, HD)] = kv_all[1, px]
+
         @pl.when(j > 0)
         def _():
             q_copy(1, 0, 1, r, dz, z_peer).wait_recv()
 
+        late = 1 - (step + len(ORDER) - LATE_FRESH) // len(ORDER)
         ahead = [
-            offset + r * part_rows + (block - holder) * rows >= 0 for holder in (p, px)
+            offset + r * part_rows + (p_block - holder) * rows - far >= 0
+            for p_block, holder, far in ((block, p, 0), (block, px, late * 2**20))
         ]
 
         query = q_all[dz, j, r]
@@ -364,60 +440,43 @@
             def _():
                 merge_for_z(chunk)
 
+        @pl.when(step == STEP_MERGE[-1])
+        def _():
+            kv_copy(1, 0, p, z_peer).start()
+
+        @pl.when(step == STEP_BLEND)
+        def _():
+            attend_late_fresh()
+            blend_group(0)
+
+        @pl.when(step == STEP_PROJECT)
+        def _():
+            project_group(0)
+
         return unused
 
     lax.fori_loop(0, len(ORDER), attend, 0)
 
     others = (to_pair, to_next, 2)
-    for k, d in ((2, to_next), (3, 2)):
-        kv_copy(k, p, x_peer(d)).start()
-    kv_copy(0, pz, z_peer).wait_recv()
-    for k, d in enumerate(others):
-        kv_copy(4 + k, pz, x_peer(d)).start()
-
-    for load in own_wo:
-        load.wait()
-    for copy in wo_copies:
-        copy.wait_recv()
-
-    def att_copy(r, core):
-        return remote(
-            att_all.at[r, core], att_all.at[r, core], att_send.at[r], att_recv.at[r], s, sib
-        )
-
-    def pr_copy(r, d):
-        back = (NY - d) % NY
-        return remote(
-            pr_out.at[r, d], pr_in.at[r, back], pr_send.at[r, d], pr_recv.at[r, back], s, y_peer(d)
-        )
-
-    per_group = CHUNKS // GROUPS
-    for g in range(GROUPS):
-        for k in range(per_group):
-            r = g * per_group + k
-            for copy in o_copies(0, r):
-                copy.wait_recv()
-            for copy in z_copies(r):
-                copy.wait_recv()
-            shares, merged = weigh([l_buf[0, 0, r], l_in[0, r], lz_in[r]])
-            for hd in range(heads):
-                att_all[g, c, pl.ds(k * part_rows, part_rows), pl.ds(hd * HD, HD)] = blend(
-                    [o_buf.at[0, 0, r], o_in.at[0, r], oz_in.at[r]], shares, hd
-                ).astype(BF16)
-        att_copy(g, c).start()
-        att_copy(g, 1 - c).wait_recv()
-        both = jnp.concatenate([att_all[g, 0], att_all[g, 1]], 1)
-        for d in (2, 1, 3):
-            part = jnp.dot(both, wo_all[(y + d) % NY], preferred_element_type=F32)
-            pr_out[g, d] = part.astype(BF16)
-            pr_copy(g, d).start()
-        own_part[g] = jnp.dot(both, wo_all[y], preferred_element_type=F32)
-
-    for d in (to_next, 2):
-        kv_copy(0, 2 * ((x + d) % NX) + zhi, z_peer).wait_recv()
-    for d in others:
-        kv_copy(0, 2 * ((x + d) % NX) + (zhi + 1) % 2, z_peer).wait_recv()
     for kind in range(2):
+        for k, d in ((2, to_next), (3, 2)):
+            kv_copy(kind, k, p, x_peer(d)).start()
+
+    def pass_on(kind):
+        kv_copy(kind, 0, pz, z_peer).wait_recv()
+        for k, d in enumerate(others):
+            kv_copy(kind, 4 + k, pz, x_peer(d)).start()
+
+    pass_on(0)
+    blend_group(1)
+    project_group(1)
+    pass_on(1)
+
+    for kind in range(2):
+        for d in (to_next, 2):
+            kv_copy(kind, 0, 2 * ((x + d) % NX) + zhi, z_peer).wait_recv()
+        for d in others:
+            kv_copy(kind, 0, 2 * ((x + d) % NX) + (zhi + 1) % 2, z_peer).wait_recv()
         for block in range(GROUP):
             fresh_pad[kind, pl.ds(slots + block * rows, rows), :] = kv_all[kind, block].astype(F32)
     start = p * slots - length
@@ -459,8 +518,9 @@
         copy.wait_send()
     for copy in pair_copies:
         copy.wait_send()
-    for k in range(7):
-        kv_copy(k, p, z_peer).wait_send()
+    for kind in range(2):
+        for k in range(7):
+            kv_copy(kind, k, p, z_peer).wait_send()
     for r in range(CHUNKS):
         for k in range(3):
             q_copy(k, 0, 0, r, 1, z_peer).wait_send()
@@ -554,8 +614,10 @@
             pltpu.VMEM((GROUPS, NY, rows // GROUPS, width), BF16),
             pltpu.VMEM((GROUPS, NY, rows // GROUPS, width), BF16),
             pltpu.VMEM((GROUPS, rows // GROUPS, width), F32),
+            pltpu.VMEM((LATE_FRESH,) + block, BF16),
+            pltpu.VMEM((LATE_FRESH, 8, HD), F32),
             dma((8,)), dma((NY,)), dma((7,)), dma((8,)), dma((NY,)), dma((NY,)), dma((2,)), dma((2,)),
-            dma((3, CHUNKS)), dma((2, 2, CHUNKS)), dma((7,)), dma((GROUP,)),
+            dma((3, CHUNKS)), dma((2, 2, CHUNKS)), dma((2, 7)), dma((2, GROUP)),
             dma((2, CHUNKS)), dma((2, CHUNKS)), dma((2, CHUNKS)), dma((2, CHUNKS)),
             dma((CHUNKS,)), dma((CHUNKS,)), dma((CHUNKS,)), dma((CHUNKS,)),
             dma((GROUPS,)), dma((GROUPS,)), dma((GROUPS, NY)), dma((GROUPS, NY)), dma((2,)),

time: 74.7 us -> 77.5 us (1.037)
  Pallas kernels: 74 us -> 76.5 us
    pallas_call x1, Pallas kernels: 71.8 us -> 74.3 us  [shards(): pl.pallas_call(kernel, out_shape=(jax.ShapeDtypeStruct((rows, width), BF1...]
where the time goes in v4:
time: 77.5 us; the launch traced here: 77.1 us
  Pallas kernels  76.5 us (99%)
    pallas_call x1, Pallas kernels, shards(): pl.pallas_call(kernel, out_shape=(jax.ShapeDtypeStruct((rows, width), BF1...  74.3 us
    pallas_call x1, Pallas kernels, shards(): pl.pallas_call(hand_on, out_shape=tuple((jax.ShapeDtypeStruct(one.shape,...  2.12 us

profile of v4, /device:TPU:1, one launch (start us, length us, event | category | flops | bytes accessed | tf_op | source)
XLA Modules:
  0.0 77.1 jit_solution(11036773671709982005)
XLA Ops:
  0.6 74.3 %span_attention.1 = (bf16[256,384]{1,0:T(8,128)(2,1)}, bf16[2048,128]{1,0:T(8,128)(2,1)}, bf16[2048,128]{1,0:T(8,128)(2,1)}) custom-call(bf16[256,384]{1,0:T(8,128)(2,1)} %tok.1, f32[8,1,384]{2,1,0:T(1,128)} %bitcast.1, bf16[3072,384]{1,0:T(8,128)(2,1)} %wq.1, bf16[3072,128]{1,0:T(8,128)(2,1)} %wk.1, bf16[3072,128]{1,0:T(8,128)(2,1)} %wv.1, ...), custom_call_target="tpu_custom_call" | custom-call | tf_op jit(solution)/shard_map/span_attention/pallas_call | solution.py:575
  75.0 2.1 %hand_on.1 = (bf16[256,384]{1,0:T(8,128)(2,1)}, bf16[2048,128]{1,0:T(8,128)(2,1)}, bf16[2048,128]{1,0:T(8,128)(2,1)}) custom-call(bf16[256,384]{1,0:T(8,128)(2,1)} %get-tuple-element.6.refs_0_, bf16[2048,128]{1,0:T(8,128)(2,1)} %get-tuple-element.7.refs_1_, bf16[2048,128]{1,0:T(8,128)(2,1)} %get-tuple-element.8.refs_2_), custom_call_target="tpu_custom_call" | custom-call | tf_op jit(solution)/shard_map/hand_on/pallas_call | solution.py:633

commit v5 on v4

--- a/solution.py
+++ b/solution.py
@@ -35,15 +35,13 @@
     return sum(d * 10**i for i, d in enumerate(digits))
 
 
-ORDER = [(0, 0, 0), (0, 0, 1), (0, 1, 0), (0, 1, 1), (1, 0, 0), (1, 1, 0), (1, 1, 1), (1, 0, 1)]
-ORDER += [(1, 1, 2), (1, 0, 2), (1, 1, 3), (1, 0, 3), (0, 1, 2), (0, 1, 3), (0, 0, 2), (0, 0, 3)]
+ORDER = [(0, 0, 0), (0, 0, 1), (0, 1, 0), (1, 0, 0), (1, 1, 0), (1, 1, 1), (1, 0, 1), (0, 1, 1)]
 LATE_FRESH = 2
-STEP_FORWARD = (4, 5, 6, 8)
-STEP_MERGE = (6, 8, 10, 11)
-STEP_KEYS = 6
-STEP_BLEND, STEP_PROJECT = 13, 14
+STEP_FORWARD = (3, 4)
+STEP_MERGE = (5, 6)
+STEP_KEYS = 0
 CHUNK = 2048
-CHUNKS = 4
+CHUNKS = 2
 GROUPS = 2
 
 
@@ -369,7 +367,8 @@
 
         @pl.when(step == STEP_KEYS)
         def _():
-            kv_copy(0, 0, p, z_peer).start()
+            for kind in range(2):
+                kv_copy(kind, 0, p, z_peer).start()
 
         @pl.when(step == LATE_FRESH)
         def _():
@@ -440,19 +439,6 @@
             def _():
                 merge_for_z(chunk)
 
-        @pl.when(step == STEP_MERGE[-1])
-        def _():
-            kv_copy(1, 0, p, z_peer).start()
-
-        @pl.when(step == STEP_BLEND)
-        def _():
-            attend_late_fresh()
-            blend_group(0)
-
-        @pl.when(step == STEP_PROJECT)
-        def _():
-            project_group(0)
-
         return unused
 
     lax.fori_loop(0, len(ORDER), attend, 0)
@@ -468,9 +454,11 @@
             kv_copy(kind, 4 + k, pz, x_peer(d)).start()
 
     pass_on(0)
-    blend_group(1)
-    project_group(1)
     pass_on(1)
+    attend_late_fresh()
+    for g in range(GROUPS):
+        blend_group(g)
+        project_group(g)
 
     for kind in range(2):
         for d in (to_next, 2):

time: 77.5 us -> 68.6 us (0.89)
  Pallas kernels: 76.5 us -> 67.9 us
    pallas_call x1, Pallas kernels: 74.3 us -> 65.8 us  [shards(): pl.pallas_call(kernel, out_shape=(jax.ShapeDtypeStruct((rows, width), BF1...]
where the time goes in v5:
time: 68.6 us; the launch traced here: 68.5 us
  Pallas kernels  67.9 us (99%)
    pallas_call x1, Pallas kernels, shards(): pl.pallas_call(kernel, out_shape=(jax.ShapeDtypeStruct((rows, width), BF1...  65.8 us
    pallas_call x1, Pallas kernels, shards(): pl.pallas_call(hand_on, out_shape=tuple((jax.ShapeDtypeStruct(one.shape,...  2.12 us

profile of v5, /device:TPU:1, one launch (start us, length us, event | category | flops | bytes accessed | tf_op | source)
XLA Modules:
  0.0 68.5 jit_solution(451722695371263343)
XLA Ops:
  0.6 65.8 %span_attention.1 = (bf16[256,384]{1,0:T(8,128)(2,1)}, bf16[2048,128]{1,0:T(8,128)(2,1)}, bf16[2048,128]{1,0:T(8,128)(2,1)}) custom-call(bf16[256,384]{1,0:T(8,128)(2,1)} %tok.1, f32[8,1,384]{2,1,0:T(1,128)} %bitcast.1, bf16[3072,384]{1,0:T(8,128)(2,1)} %wq.1, bf16[3072,128]{1,0:T(8,128)(2,1)} %wk.1, bf16[3072,128]{1,0:T(8,128)(2,1)} %wv.1, ...), custom_call_target="tpu_custom_call" | custom-call | tf_op jit(solution)/shard_map/span_attention/pallas_call | solution.py:563
  66.4 2.1 %hand_on.1 = (bf16[256,384]{1,0:T(8,128)(2,1)}, bf16[2048,128]{1,0:T(8,128)(2,1)}, bf16[2048,128]{1,0:T(8,128)(2,1)}) custom-call(bf16[256,384]{1,0:T(8,128)(2,1)} %get-tuple-element.6.refs_0_, bf16[2048,128]{1,0:T(8,128)(2,1)} %get-tuple-element.7.refs_1_, bf16[2048,128]{1,0:T(8,128)(2,1)} %get-tuple-element.8.refs_2_), custom_call_target="tpu_custom_call" | custom-call | tf_op jit(solution)/shard_map/hand_on/pallas_call | solution.py:621

commit v6 on v5

--- a/solution.py
+++ b/solution.py
@@ -39,7 +39,7 @@
 LATE_FRESH = 2
 STEP_FORWARD = (3, 4)
 STEP_MERGE = (5, 6)
-STEP_KEYS = 0
+STEP_KEYS = 4
 CHUNK = 2048
 CHUNKS = 2
 GROUPS = 2
@@ -108,8 +108,8 @@
         for yy in range(NY)
     ]
     barrier = pltpu.get_barrier_semaphore()
-    peers = [(s, sib), (z_peer, h)]
-    peers += [(s, y_peer(d)) for d in (1, 2, 3)] + [(x_peer(d), h) for d in (1, 2, 3)]
+    peers = [(z_peer, h), (s, y_peer(2)), (x_peer(2), h)]
+    peers += [(s, y_peer(d)) for d in (1, 3)] + [(x_peer(d), h) for d in (1, 3)] + [(s, sib)]
     for seq, head in peers:
         pl.semaphore_signal(
             barrier, inc=1, device_id=(seq, head), device_id_type=pl.DeviceIdType.MESH
@@ -208,13 +208,6 @@
             kv_send.at[kind, k], kv_recv.at[kind, block], seq, h,
         )
 
-    fresh_key = rope(acc[:, pl.ds(width, HD)] * scale).astype(BF16)
-    fresh_value = (acc[:, pl.ds(width + HD, HD)] * scale).astype(BF16)
-    kv_all[0, p] = fresh_key
-    kv_all[1, p] = fresh_value
-    for kind in range(2):
-        kv_copy(kind, 1, p, x_peer(to_pair)).start()
-
     def q_copy(k, dz, j, r, to_z, seq):
         return remote(
             q_all.at[dz, 0, r], q_all.at[to_z, j, r], q_send.at[k, r], q_recv.at[to_z, j, r], seq, h
@@ -229,6 +222,12 @@
             q_all[0, 0, r, pl.ds(hd * part_rows, part_rows), :] = (turned * fold).astype(BF16)
         q_copy(0, 0, 0, r, 1, z_peer).start()
         q_copy(1, 0, 1, r, 0, x_peer(to_next)).start()
+    fresh_key = rope(acc[:, pl.ds(width, HD)] * scale).astype(BF16)
+    fresh_value = (acc[:, pl.ds(width + HD, HD)] * scale).astype(BF16)
+    kv_all[0, p] = fresh_key
+    kv_all[1, p] = fresh_value
+    for kind in range(2):
+        kv_copy(kind, 1, p, x_peer(to_pair)).start()
     for copy in wo_copies:
         copy.start()
 

time: 68.6 us -> 68.8 us (level)
  no operation moved by 1% of the time
where the time goes in v6:
time: 68.8 us; the launch traced here: 68.7 us
  Pallas kernels  68.1 us (99%)
    pallas_call x1, Pallas kernels, shards(): pl.pallas_call(kernel, out_shape=(jax.ShapeDtypeStruct((rows, width), BF1...  65.9 us
    pallas_call x1, Pallas kernels, shards(): pl.pallas_call(hand_on, out_shape=tuple((jax.ShapeDtypeStruct(one.shape,...  2.12 us

profile of v6, /device:TPU:1, one launch (start us, length us, event | category | flops | bytes accessed | tf_op | source)
XLA Modules:
  0.0 68.7 jit_solution(2987945559838048554)
XLA Ops:
  0.6 65.9 %span_attention.1 = (bf16[256,384]{1,0:T(8,128)(2,1)}, bf16[2048,128]{1,0:T(8,128)(2,1)}, bf16[2048,128]{1,0:T(8,128)(2,1)}) custom-call(bf16[256,384]{1,0:T(8,128)(2,1)} %tok.1, f32[8,1,384]{2,1,0:T(1,128)} %bitcast.1, bf16[3072,384]{1,0:T(8,128)(2,1)} %wq.1, bf16[3072,128]{1,0:T(8,128)(2,1)} %wk.1, bf16[3072,128]{1,0:T(8,128)(2,1)} %wv.1, ...), custom_call_target="tpu_custom_call" | custom-call | tf_op jit(solution)/shard_map/span_attention/pallas_call | solution.py:562
  66.6 2.1 %hand_on.1 = (bf16[256,384]{1,0:T(8,128)(2,1)}, bf16[2048,128]{1,0:T(8,128)(2,1)}, bf16[2048,128]{1,0:T(8,128)(2,1)}) custom-call(bf16[256,384]{1,0:T(8,128)(2,1)} %get-tuple-element.6.refs_0_, bf16[2048,128]{1,0:T(8,128)(2,1)} %get-tuple-element.7.refs_1_, bf16[2048,128]{1,0:T(8,128)(2,1)} %get-tuple-element.8.refs_2_), custom_call_target="tpu_custom_call" | custom-call | tf_op jit(solution)/shard_map/hand_on/pallas_call | solution.py:620

commit v7 on v6

--- a/solution.py
+++ b/solution.py
@@ -35,10 +35,10 @@
     return sum(d * 10**i for i, d in enumerate(digits))
 
 
-ORDER = [(0, 0, 0), (0, 0, 1), (0, 1, 0), (1, 0, 0), (1, 1, 0), (1, 1, 1), (1, 0, 1), (0, 1, 1)]
+ORDER = [(0, 0, 0), (0, 0, 1), (1, 0, 0), (1, 1, 0), (1, 1, 1), (1, 0, 1), (0, 1, 0), (0, 1, 1)]
 LATE_FRESH = 2
-STEP_FORWARD = (3, 4)
-STEP_MERGE = (5, 6)
+STEP_FORWARD = (2, 3)
+STEP_MERGE = (4, 5)
 STEP_KEYS = 4
 CHUNK = 2048
 CHUNKS = 2

time: 68.8 us -> 70.4 us (1.023); the launches traced: 68.7 us -> 69.1 us
  no operation moved by 1% of the time
where the time goes in v7:
time: 70.4 us; the launch traced here: 69.1 us
  Pallas kernels  68.4 us (97%)
    pallas_call x1, Pallas kernels, shards(): pl.pallas_call(kernel, out_shape=(jax.ShapeDtypeStruct((rows, width), BF1...  66.3 us
    pallas_call x1, Pallas kernels, shards(): pl.pallas_call(hand_on, out_shape=tuple((jax.ShapeDtypeStruct(one.shape,...  2.12 us

profile of v7, /device:TPU:1, one launch (start us, length us, event | category | flops | bytes accessed | tf_op | source)
XLA Modules:
  0.0 69.1 jit_solution(8263352966132814614)
XLA Ops:
  0.6 66.3 %span_attention.1 = (bf16[256,384]{1,0:T(8,128)(2,1)}, bf16[2048,128]{1,0:T(8,128)(2,1)}, bf16[2048,128]{1,0:T(8,128)(2,1)}) custom-call(bf16[256,384]{1,0:T(8,128)(2,1)} %tok.1, f32[8,1,384]{2,1,0:T(1,128)} %bitcast.1, bf16[3072,384]{1,0:T(8,128)(2,1)} %wq.1, bf16[3072,128]{1,0:T(8,128)(2,1)} %wk.1, bf16[3072,128]{1,0:T(8,128)(2,1)} %wv.1, ...), custom_call_target="tpu_custom_call" | custom-call | tf_op jit(solution)/shard_map/span_attention/pallas_call | solution.py:562
  66.9 2.1 %hand_on.1 = (bf16[256,384]{1,0:T(8,128)(2,1)}, bf16[2048,128]{1,0:T(8,128)(2,1)}, bf16[2048,128]{1,0:T(8,128)(2,1)}) custom-call(bf16[256,384]{1,0:T(8,128)(2,1)} %get-tuple-element.6.refs_0_, bf16[2048,128]{1,0:T(8,128)(2,1)} %get-tuple-element.7.refs_1_, bf16[2048,128]{1,0:T(8,128)(2,1)} %get-tuple-element.8.refs_2_), custom_call_target="tpu_custom_call" | custom-call | tf_op jit(solution)/shard_map/hand_on/pallas_call | solution.py:620
